TPU v7x, 256 devices: a whole 4x4x8 slice. The times are simulated.
256 devices in a mesh: box: 64 (over y, z, core), rank: 4 (over x).
Axes of the slice: x: 4, y: 4, z: 8, core: 2. Of those that a mesh axis runs over, the one named last changes fastest.
Arguments:
- coeffs: float32 [1000, 16384], P(None, 'box'), may hold values from -6 to 6
- operator: float32 [12, 3, 3, 10, 10], P('rank'), may hold values from -1 to 1
- filters: float32 [2, 10, 10], replicated, may hold values from -2 to 2
- neighbours: int32 [7, 16384], P(None, 'box'), may hold values from -1 to 16383, as said below
- parent_one: int32 [16384], P('box'), may hold values from -1 to 2047, as said below
- octant_one: int32 [16384], P('box'), may hold values from 0 to 7, as said below
- parent_two: int32 [2048], P('box'), may hold values from -1 to 255, as said below
- octant_two: int32 [2048], P('box'), may hold values from 0 to 7, as said below
- keep: int32 [16384], P('box'), may hold values 0 or 1
Outputs:
- leaves: float32 [1000, 16384], P(None, 'box')
- level_one: float32 [1000, 2048], P(None, 'box')
- level_two: float32 [1000, 256], P(None, 'box')
Inputs may be any that keep to these rules, and one draw needn't show every extreme that they name: Leaf boxes tile 160 cubes of 4 x 4 x 4 laid along x, in Morton order within each cube and cube after cube; each index of box holds a contiguous run of them in its first slots, between 64 and 256 boxes, and some index holds 256. neighbours[e, s] is the slot of the face neighbour of the box in slot s at displacement e, -1 where slot s is empty or the neighbour lies outside the domain; a neighbour on another index lies on the next one within its first 64 slots, or on the previous one within its last 64 occupied slots. `parent_one`: A parent is held by the index of box that holds its first child, in the order of its parents; only the first seven leaves of an index can have a parent on another index, and then it is the last parent of the previous index. -1 marks empty slots. `octant_one`: bits 0, 1, 2 tell whether the box is the upper child along x, y, z; 0 in empty slots. `parent_two`: likewise one level up: only the first seven level-one boxes of an index can have a parent on another index, and then it is the last parent of the previous index. -1 marks empty slots. `octant_two`: bits 0, 1, 2 tell whether the box is the upper child along x, y, z; 0 in empty slots.
All inputs are finite; a program needn't handle non-finite values. No bound on the sum of `keep` on one device may be relied on, other than what follows from the above.
Results may differ from a plain program's by a relative error of at most 0.00013.
Values sent between devices are 32-bit elements; how exact they have to be, the bound alone decides.
No kernel may reach another device: no remote copies, remote signals or barrier semaphores. Data moves between devices by JAX's collectives and lax.ppermute only.
A program may use at most 128 MiB of HBM per device.

v0:
```python
import jax
import jax.numpy as jnp
import numpy as np
from jax import lax
from jax.experimental import pallas as pl
from jax.experimental.pallas import tpu as pltpu
from jax.sharding import PartitionSpec as P

F32 = jnp.float32
BF16 = jnp.bfloat16
I32 = jnp.int32
HIGHEST_MODE = lax.Precision.HIGHEST
CHILD_SCALE = 8.0 ** (-0.5)

K = 10
SQ = 100
KKK = 1000
CAP = 256
EDGE = 64
HALF = 504
LANES = 128
KT = 60
MROWS = 1008
GROUPS = 6

SAME_X = (0, 3, 4, 5, 6)
Y_CODE = {0: 0, 3: 1, 4: 2, 5: 0, 6: 0}
Z_CODE = {0: 0, 3: 0, 4: 0, 5: 1, 6: 2}


def split(value):
    high = value.astype(BF16)
    low = (value - high.astype(F32)).astype(BF16)
    return high, low


def mm(a, b):
    return jnp.dot(a, b, preferred_element_type=F32)


def mm_t(a, b):
    return lax.dot_general(a, b, (((1,), (1,)), ((), ())), preferred_element_type=F32)


def mm_full(a, b):
    return jnp.dot(a, b, preferred_element_type=F32, precision=HIGHEST_MODE)


def iota(shape, dim):
    return lax.broadcasted_iota(I32, shape, dim)


def tenth(index):
    return jnp.floor((index.astype(F32) + 0.5) * 0.1).astype(I32)


def edges_kernel(x_ref, nb_ref, head_ref, tail_ref):
    count = jnp.sum((nb_ref[0:1, :] >= 0).astype(F32), axis=1, keepdims=True)
    row = iota((2 * CAP, 2 * LANES), 0)
    lane = iota((2 * CAP, 2 * LANES), 1)
    slot = row & (CAP - 1)
    same_half = (row >= CAP) == ((lane & (LANES - 1)) >= EDGE)
    column = lane & (EDGE - 1)
    wanted = jnp.where(lane < LANES, column, column - EDGE + count.astype(I32))
    pick = ((slot == wanted) & same_half).astype(F32).astype(BF16)
    top_high, top_low = split(x_ref[0:HALF, :])
    below = jnp.concatenate([x_ref[HALF:KKK, :], jnp.zeros((2 * HALF - KKK, CAP), F32)], axis=0)
    low_high, low_low = split(below)
    both = mm(top_high, pick[:CAP]) + mm(top_low, pick[:CAP])
    both = both + (mm(low_high, pick[CAP:]) + mm(low_low, pick[CAP:]))
    head_ref[...] = both[:, :LANES]
    spot = (iota((HALF, LANES), 0) == HALF - 1) & (iota((HALF, LANES), 1) >= EDGE)
    tail_ref[...] = jnp.where(spot, count, both[:, LANES:])


def compress(value_ref, select, ff_high, ff_low, filter_smem, work_ref, out_ref):
    high, low = split(value_ref[0:KKK, :])
    span = KKK + 32
    for w in range(4):
        part = select[w * LANES : (w + 1) * LANES]
        work_ref[w * span : w * span + KKK, :] = mm_t(high, part) + mm_t(low, part)
        work_ref[w * span + KKK : (w + 1) * span, :] = jnp.zeros((32, LANES), F32)
    base = 4 * span
    for pair in range(5):
        columns = []
        for i in (2 * pair, 2 * pair + 1):
            columns.append(
                jnp.concatenate(
                    [work_ref[w * span + i * SQ : w * span + i * SQ + LANES, :] for w in range(4)],
                    axis=0,
                )
            )
        rhs_high, rhs_low = split(jnp.concatenate(columns, axis=1))
        z = mm(ff_high, rhs_high) + mm(ff_low, rhs_high) + mm(ff_high, rhs_low)
        work_ref[base + 208 * pair : base + 208 * pair + 104, :] = z[:, :LANES]
        work_ref[base + 208 * pair + 104 : base + 208 * pair + 208, :] = z[:, LANES:]
    upper = iota((1, LANES), 1) >= 64
    for a in range(K):
        total = None
        for i in range(K):
            weight = jnp.where(upper, filter_smem[1, a, i], filter_smem[0, a, i]) * CHILD_SCALE
            term = work_ref[base + 104 * i : base + 104 * i + 104, :] * weight
            total = term if total is None else total + term
        total = total + pltpu.roll(total, 64, axis=1)
        out_ref[a * SQ : (a + 1) * SQ, :] = total[:SQ]


def main_kernel(
    x_ref,
    left_ref,
    right_ref,
    op0_ref,
    op1_ref,
    op2_ref,
    op3_ref,
    ints_ref,
    cols_ref,
    filter_ref,
    filter_smem,
    leaves_ref,
    one_ref,
    two_ref,
    send_ref,
    w_high,
    w_low,
    stage,
    s_high,
    s_low,
    s_stage,
    x_pad,
    edge,
    picks,
    b_wide,
    c_wide,
    ops,
    acc_ref,
    applied,
    level,
    level_up,
):
    ops[...] = jnp.zeros_like(ops)
    for n, ref in enumerate((op0_ref, op1_ref, op2_ref, op3_ref)):
        ops[3 * n : 3 * n + 3, 0:900] = ref[...]
    factors = ops[...]
    row = iota((104, LANES), 0)
    lane = iota((104, LANES), 1)
    spread = jnp.where(row < 80, (row >> 3) * 10 + (row & 7), 0)
    spread = jnp.where((row >= 80) & (row < 88), (row - 80) * 10 + 8, spread)
    spread = jnp.where((row >= 88) & (row < 96), (row - 88) * 10 + 9, spread)
    spread = jnp.where(row >= 96, 80 + ((row - 96) >> 1) * 10 + 8 + (row & 1), spread)
    order = ((spread == lane) & (row < 100)).astype(F32).astype(BF16)
    x_factor = []
    for code in range(3):
        moved = factors if code == 0 else pltpu.roll(factors, 1024 - SQ * code, axis=1)
        high, low = split(moved[:, :LANES])
        x_factor.append(mm_t(order, jnp.concatenate([high, low, high], axis=0)).astype(BF16))
    x_same = x_factor[0]
    x_moved = jnp.concatenate([x_factor[1], x_factor[2]], axis=0)
    column_of = iota((384, 512), 0)
    y_cols = (column_of == cols_ref[0:1, :]).astype(F32)
    z_cols = (column_of == cols_ref[1:2, :]).astype(F32)
    y_rows = [pltpu.roll(factors, 1024 - 300 - 10 * b, axis=1)[:, :384] for b in range(K)]
    z_rows = [pltpu.roll(factors, 1024 - 600 - 10 * b, axis=1)[:, :384] for b in range(K)]
    b_wide[...] = mm_full(jnp.concatenate(y_rows, axis=0), y_cols).reshape(K, 16, 512)
    c_wide[...] = mm_full(jnp.concatenate(z_rows, axis=0), z_cols).reshape(K, 16, 512)

    def build(pair_of, count, width):
        step = width // K if width == 160 else 4

        def put(value, first_tile, position, tiles):
            for l in range(tiles):
                t = first_tile + l
                part = value[:, l * LANES : (l + 1) * LANES]
                for a in range(K):
                    stage[pl.ds(t * width + a * step + position, 8, stride=6 * width), :] = part[
                        8 * a : 8 * a + 8
                    ]
                for n, i in enumerate((8, 9)):
                    stage[
                        pl.ds((i * 6 + t) * width + position, 8, stride=step), :
                    ] = part[80 + 8 * n : 88 + 8 * n]
                for n, a in enumerate((8, 9)):
                    stage[
                        pl.ds((48 + t) * width + a * step + position, 2, stride=6 * width), :
                    ] = part[96 + 2 * n : 98 + 2 * n]

        held = []
        for u in range(count):
            b, c = pair_of(u)
            high, low = split(b_wide[b] * c_wide[c])
            rhs = jnp.concatenate([high, high, low], axis=0)
            for half in range(2):
                put(mm(x_same, rhs[:, 256 * half : 256 * half + 256]), 2 * half, u, 2)
            held.append(rhs[:, :LANES])
            if len(held) == 2:
                both = mm(x_moved, jnp.concatenate(held, axis=1))
                for n in range(2):
                    put(both[:104, n * LANES : (n + 1) * LANES], 4, u - 1 + n, 1)
                    put(both[104:, n * LANES : (n + 1) * LANES], 5, u - 1 + n, 1)
                held = []

    def one_group(g, carry):
        def pair_of(u):
            p = g * 16 + u
            b = (p * 205) >> 11
            return b, p - 10 * b

        build(pair_of, 16, 160)
        first = pl.multiple_of(g * 160, 160)
        for t in range(KT):
            high, low = split(stage[t * 160 : (t + 1) * 160, :])
            w_high[pl.ds(first, 160), t * LANES : (t + 1) * LANES] = high
            w_low[pl.ds(first, 160), t * LANES : (t + 1) * LANES] = low
        return carry

    lax.fori_loop(0, GROUPS, one_group, 0)
    stage[0 : KT * 48, :] = jnp.zeros((KT * 48, LANES), F32)
    build(lambda u: (9, 6 + u), 4, 48)
    for t in range(KT):
        high, low = split(stage[t * 48 : (t + 1) * 48, :])
        w_high[960:MROWS, t * LANES : (t + 1) * LANES] = high
        w_low[960:MROWS, t * LANES : (t + 1) * LANES] = low

    first_half = iota((HALF, LANES), 1) < EDGE
    left = left_ref[...]
    right = right_ref[...]
    edge[0:HALF, :] = jnp.where(first_half, left, pltpu.roll(right, EDGE, axis=1))
    edge[HALF : 2 * HALF, :] = jnp.where(first_half, pltpu.roll(left, EDGE, axis=1), right)
    for i in range(K):
        x_pad[112 * i : 112 * i + SQ, 0:CAP] = x_ref[SQ * i : SQ * i + SQ, :]
        x_pad[112 * i : 112 * i + SQ, CAP : CAP + LANES] = edge[SQ * i : SQ * i + SQ, :]
        x_pad[112 * i + SQ : 112 * i + 112, :] = jnp.zeros((12, CAP + LANES), F32)
    near = ints_ref[0:8, :]
    origin = near[0:1, 0:1]
    before = left[HALF - 1 : HALF, EDGE : EDGE + 1].astype(I32)
    moved = near - origin
    place = jnp.where(moved < 0, moved + (2 * CAP + EDGE) - before, moved)
    place = jnp.where(moved >= CAP, moved + EDGE, place)
    place = jnp.where(near >= 0, place, -1)
    live = (near[0:1, :] >= 0).astype(F32)
    slots = iota((CAP + LANES, CAP), 0)
    for e in range(1, 7):
        picks[e - 1] = (slots == place[e : e + 1, :]).astype(F32).astype(BF16)
    s_stage[500:512, :] = jnp.zeros((12, CAP), F32)
    s_stage[612:640, :] = jnp.zeros((28, CAP), F32)
    s_stage[740:768, :] = jnp.zeros((28, CAP), F32)

    def one_i(i, carry):
        rows = x_pad[pl.ds(pl.multiple_of(i * 112, 112), 112), :]
        high, low = split(rows)
        wide = jnp.concatenate(
            [high[:, :CAP], low[:, :CAP], high[:, CAP:], low[:, CAP:]], axis=1
        )
        s_stage[0:SQ, :] = rows[:SQ, :CAP] * live
        for e in range(1, 7):
            pick = picks[e - 1]
            near_pick = pick[:CAP]
            far_pick = pick[CAP:]
            taken = mm(
                wide, jnp.concatenate([near_pick, near_pick, far_pick, far_pick], axis=0)
            )
            at = 512 if e == 1 else 640 if e == 2 else SQ * (e - 2)
            s_stage[at : at + SQ, :] = taken[:SQ]
        high, low = split(s_stage[...])
        at = pl.multiple_of(i * 768, 768)
        s_high[pl.ds(at, 768), :] = high
        s_low[pl.ds(at, 768), :] = low
        return carry

    lax.fori_loop(0, K, one_i, 0)

    acc_ref[...] = mm(w_high[...], s_high[...])
    acc_ref[...] += mm(w_low[...], s_high[...])
    acc_ref[...] += mm(w_high[...], s_low[...])
    for a in range(K):
        for g in range(GROUPS):
            applied[a * SQ + 16 * g : a * SQ + 16 * g + 16, :] = acc_ref[
                g * 160 + a * 16 : g * 160 + a * 16 + 16, :
            ]
        applied[a * SQ + 96 : a * SQ + SQ, :] = acc_ref[960 + 4 * a : 964 + 4 * a, :]
    leaves_ref[...] = applied[...] * ints_ref[10:11, :].astype(F32)

    p_row = iota((104, 16), 0)
    small = iota((104, 16), 1)
    b_of = tenth(p_row)
    c_of = p_row - 10 * b_of
    pick_b = ((b_of == small) & (p_row < SQ)).astype(F32)
    pick_c = ((c_of == small) & (p_row < SQ)).astype(F32)
    q_lane = iota((16, LANES), 1)
    j_of = tenth(q_lane)
    k_of = q_lane - 10 * j_of
    small = iota((16, LANES), 0)
    pick_j = ((j_of == small) & (q_lane < SQ)).astype(F32)
    pick_k = ((k_of == small) & (q_lane < SQ)).astype(F32)
    y_filter = []
    z_filter = []
    for f in range(2):
        level_up[0:16, :] = jnp.zeros((16, LANES), F32)
        level_up[0:K, 0:K] = filter_ref[f]
        square = level_up[0:16, :]
        left_b = mm_full(pick_b, square)
        left_c = mm_full(pick_c, square)
        grown = jnp.zeros((112, LANES), F32)
        wide_j = jnp.concatenate([pick_j, grown], axis=0)
        wide_k = jnp.concatenate([pick_k, grown], axis=0)
        y_filter.append(mm_full(left_b, wide_j))
        z_filter.append(mm_full(left_c, wide_k))
    ff = jnp.concatenate(
        [y_filter[0] * z_filter[0], y_filter[1] * z_filter[0], y_filter[0] * z_filter[1], y_filter[1] * z_filter[1]],
        axis=1,
    )
    ff_high, ff_low = split(ff)
    parent = ints_ref[8:9, :]
    octant = ints_ref[9:10, :]
    local = parent - (origin >> 3)
    local = jnp.where(local < 0, 32, local)
    code = (octant >> 1) * LANES + (octant & 1) * 64 + local
    code = jnp.where(parent >= 0, code, -1)
    rows = iota((4 * LANES, CAP), 0)
    select = (rows == code).astype(F32).astype(BF16)
    compress(applied, select, ff_high, ff_low, filter_smem, stage, level)
    parent = ints_ref[11:12, 0:LANES]
    octant = ints_ref[12:13, 0:LANES]
    lane = iota((1, LANES), 1)
    local = parent - (origin >> 6)
    local = jnp.where(local < 0, 4, local)
    code = (octant >> 1) * LANES + (octant & 1) * 64 + local
    code = jnp.where((parent >= 0) & (lane < 32), code, -1)
    last = (octant[:, 0:1] + 7) & 7
    code = jnp.where(lane == 32, (last >> 1) * LANES + (last & 1) * 64 + 4, code)
    rows = iota((4 * LANES, LANES), 0)
    select = (rows == code).astype(F32).astype(BF16)
    compress(level, select, ff_high, ff_low, filter_smem, stage, level_up)
    one_ref[...] = level[:, 0:32]
    two_ref[...] = level_up[:, 0:4]
    row = iota((8, LANES), 0)
    lane = iota((8, LANES), 1)
    pick_one = ((row == 0) & (lane == 32)).astype(F32)
    pick_two = ((row == 1) & (lane == 4)).astype(F32)
    sent = lax.dot_general(
        pick_one, level[...], (((1,), (1,)), ((), ())), preferred_element_type=F32, precision=HIGHEST_MODE
    ) + lax.dot_general(
        pick_two, level_up[...], (((1,), (1,)), ((), ())), preferred_element_type=F32, precision=HIGHEST_MODE
    )
    send_ref[...] = sent


def column_table():
    table = np.full((8, 512), -1, np.int32)
    for n, e in enumerate(SAME_X):
        for j in range(K):
            for k in range(K):
                at = n * SQ + j * K + k
                table[0, at] = Y_CODE[e] * SQ + j
                table[1, at] = Z_CODE[e] * SQ + k
    return table


VMEM_SPEC = pl.BlockSpec(memory_space=pltpu.VMEM)
SMEM_SPEC = pl.BlockSpec(memory_space=pltpu.SMEM)
PARAMS = pltpu.CompilerParams(vmem_limit_bytes=63 * 1024 * 1024)


def shape(dims, dtype=F32):
    return jax.ShapeDtypeStruct(dims, dtype)


def edges(coeffs, neighbours):
    return pl.pallas_call(
        edges_kernel,
        out_shape=(shape((HALF, LANES)), shape((HALF, LANES))),
        in_specs=[VMEM_SPEC] * 2,
        out_specs=(VMEM_SPEC,) * 2,
        name="edges",
    )(coeffs, neighbours)


def gather_ints(neighbours, parent_one, octant_one, parent_two, octant_two, keep):
    wide = lambda v: jnp.pad(v, (0, CAP - v.shape[0]))[None]
    blank = jnp.full((1, CAP), -1, I32)
    rows = [neighbours, blank, parent_one[None], octant_one[None], keep[None]]
    rows += [wide(parent_two), wide(octant_two), blank, blank, blank]
    return jnp.concatenate(rows, axis=0)


def operator_step(coeffs, from_left, from_right, terms, ints, filters):
    return pl.pallas_call(
        main_kernel,
        out_shape=(shape((KKK, CAP)), shape((KKK, 32)), shape((KKK, 4)), shape((8, KKK))),
        in_specs=[VMEM_SPEC] * 10 + [SMEM_SPEC],
        out_specs=(VMEM_SPEC,) * 4,
        scratch_shapes=[
            pltpu.VMEM((MROWS, KT * LANES), BF16),
            pltpu.VMEM((MROWS, KT * LANES), BF16),
            pltpu.VMEM((KT * 160, LANES), F32),
            pltpu.VMEM((KT * LANES, CAP), BF16),
            pltpu.VMEM((KT * LANES, CAP), BF16),
            pltpu.VMEM((768, CAP), F32),
            pltpu.VMEM((1120, CAP + LANES), F32),
            pltpu.VMEM((2 * HALF, LANES), F32),
            pltpu.VMEM((6, CAP + LANES, CAP), BF16),
            pltpu.VMEM((K, 16, 512), F32),
            pltpu.VMEM((K, 16, 512), F32),
            pltpu.VMEM((16, 1024), F32),
            pltpu.VMEM((MROWS, CAP), F32),
            pltpu.VMEM((KKK, CAP), F32),
            pltpu.VMEM((KKK, LANES), F32),
            pltpu.VMEM((KKK, LANES), F32),
        ],
        compiler_params=PARAMS,
        name="operator",
    )(coeffs, from_left, from_right, *terms, ints, jnp.asarray(column_table()), filters, filters)


def per_device(
    coeffs, operator, filters, neighbours, parent_one, octant_one, parent_two, octant_two, keep
):
    terms = operator.reshape(3, 900)
    others = [
        lax.ppermute(terms, "rank", [(i, (i + step) % 4) for i in range(4)]) for step in (1, 2, 3)
    ]
    head, tail = edges(coeffs, neighbours)
    count = lax.axis_size("box")
    from_left = lax.ppermute(tail, "box", [(i, i + 1) for i in range(count - 1)])
    from_right = lax.ppermute(head, "box", [(i + 1, i) for i in range(count - 1)])
    ints = gather_ints(neighbours, parent_one, octant_one, parent_two, octant_two, keep)
    leaves, level_one, level_two, sent = operator_step(
        coeffs, from_left, from_right, (terms, *others), ints, filters
    )
    received = lax.ppermute(sent[:2], "box", [(i + 1, i) for i in range(count - 1)])
    me = lax.axis_index("box")
    slots_one = jnp.arange(level_one.shape[1])
    slots_two = jnp.arange(level_two.shape[1])
    last_one = jnp.max(parent_one) - me * level_one.shape[1]
    last_two = jnp.max(parent_two) - me * level_two.shape[1]
    level_one = level_one + received[0][:, None] * (slots_one == last_one)[None, :].astype(F32)
    level_two = level_two + received[1][:, None] * (slots_two == last_two)[None, :].astype(F32)
    return leaves, level_one, level_two


def solution(mesh):
    placed = (
        P(None, "box"),
        P("rank", None, None, None, None),
        P(),
        P(None, "box"),
        P("box"),
        P("box"),
        P("box"),
        P("box"),
        P("box"),
    )
    return jax.shard_map(
        per_device,
        mesh=mesh,
        in_specs=placed,
        out_specs=(P(None, "box"), P(None, "box"), P(None, "box")),
        check_vma=False,
    )
```

profile of v0, /device:TPU:25, one launch (start us, length us, event | category | flops | bytes accessed | tf_op | source)
XLA Modules:
  0.0 95.9 jit_solution(17738808975229860531)
XLA Ops:
  0.6 2.6 %edges.1 = (f32[504,128]{1,0:T(8,128)}, f32[504,128]{1,0:T(8,128)}) custom-call(f32[1000,256]{1,0:T(8,128)} %x_ref.3, s32[7,256]{1,0:T(8,128)} %nb_ref.1), custom_call_target="tpu_custom_call" | custom-call | tf_op jit(solution)/shard_map/edges/pallas_call | solution.py:369
  3.2 4.1 %collective-permute-start = (f32[504,128]{1,0:T(8,128)}, f32[504,128]{1,0:T(8,128)S(1)}, u32[]{:S(2)}, u32[]{:S(2)}) collective-permute-start(f32[504,128]{1,0:T(8,128)} %get-tuple-element.9), channel_id=1, source_target_pairs={{0,4},{4,8},{8,12},{12,16},{16,20},{20,24},{24,28},{28,32},{32,36}... | collective-permute-start | bytes 774152 | tf_op jit(solution)/shard_map/ppermute | solution.py:424
  7.3 1.9 %collective-permute-start.1 = (f32[504,128]{1,0:T(8,128)}, f32[504,128]{1,0:T(8,128)S(1)}, u32[]{:S(2)}, u32[]{:S(2)}) collective-permute-start(f32[504,128]{1,0:T(8,128)} %get-tuple-element.10), channel_id=1, source_target_pairs={{4,0},{8,4},{12,8},{16,12},{20,16},{24,20},{28,24},{32,28},{36,32}... | collective-permute-start | bytes 774152 | tf_op jit(solution)/shard_map/ppermute | solution.py:425
  9.3 0.0 copy-start.13
  9.3 0.1 reshape.23.op0_ref
  9.4 0.0 copy-start.4
  9.4 0.0 copy-start.9
  9.5 1.3 %collective-permute-start.2 = (f32[3,900]{1,0:T(4,128)S(1)}, f32[3,900]{1,0:T(4,128)S(1)}, u32[]{:S(2)}, u32[]{:S(2)}) collective-permute-start(f32[3,900]{1,0:T(4,128)S(1)} %reshape.23.op0_ref), channel_id=1, source_target_pairs={{0,1},{1,2},{2,3},{3,0},{4,5},{5,6},{6,7},{7,4},{8,9},{9,10},{10,1... | collective-permute-start | bytes 32408 | tf_op jit(solution)/shard_map/ppermute | solution.py:420
  10.7 2.5 %collective-permute-start.3 = (f32[3,900]{1,0:T(4,128)S(1)}, f32[3,900]{1,0:T(4,128)S(1)}, u32[]{:S(2)}, u32[]{:S(2)}) collective-permute-start(f32[3,900]{1,0:T(4,128)S(1)} %reshape.23.op0_ref), channel_id=1, source_target_pairs={{0,2},{1,3},{2,0},{3,1},{4,6},{5,7},{6,4},{7,5},{8,10},{9,11},{10,... | collective-permute-start | bytes 32408 | tf_op jit(solution)/shard_map/ppermute | solution.py:420
  13.2 1.2 %collective-permute-start.4 = (f32[3,900]{1,0:T(4,128)S(1)}, f32[3,900]{1,0:T(4,128)S(1)}, u32[]{:S(2)}, u32[]{:S(2)}) collective-permute-start(f32[3,900]{1,0:T(4,128)S(1)} %reshape.23.op0_ref), channel_id=1, source_target_pairs={{0,3},{1,0},{2,1},{3,2},{4,7},{5,4},{6,5},{7,6},{8,11},{9,8},{10,9... | collective-permute-start | bytes 32408 | tf_op jit(solution)/shard_map/ppermute | solution.py:420
  14.4 0.6 reduce_max.19
  15.7 0.0 copy-start.14
  15.7 0.6 copy-done.14
  16.3 0.6 copy.19.filter_ref.filter_smem
  16.9 0.7 copy-done.10
  17.6 0.6 reduce_max.18
  18.9 0.6 copy-done.5
  19.6 1.2 %concatenate.7.ints_ref = s32[16,256]{1,0:T(8,128)} concatenate(s32[7,256]{1,0:T(8,128)S(1)} %copy-done.5, s32[1,256]{1,0:T(1,128)S(1)} %broadcast_in_dim.20, s32[1,256]{1,0:T(1,128)S(1)} %bitcast.9, s32[1,256]{1,0:T(1,128)S(1)} %bitcast.12, s32[1,256]{1,0:T(1,128)S(1)} %bitcast.13, s32[1,256]{1,0:T(1,128)S(1)} %bitcast.10, s32[1,256]{1,0:T(1,128)S(1)} %bitcast.11, ...), dimensions={0} | concatenate | bytes 32768 | tf_op jit(solution)/shard_map/concatenate | solution.py:383
  20.9 0.5 copy-done.6
  21.4 0.0 copy-done.7
  21.4 0.0 copy-done.8
  21.4 0.1 copy-done.1
  21.6 0.7 copy-done.2
  22.2 62.1 %operator.1 = (f32[1000,256]{1,0:T(8,128)}, f32[1000,32]{1,0:T(8,128)}, f32[1000,4]{1,0:T(8,128)}, f32[8,1000]{1,0:T(8,128)}) custom-call(f32[1000,256]{1,0:T(8,128)} %x_ref.3, f32[504,128]{1,0:T(8,128)} %copy-done.1, f32[504,128]{1,0:T(8,128)} %copy-done.2, f32[3,900]{1,0:T(4,128)} %copy-done.4, f32[3,900]{1,0:T(4,128)} %copy-done.6, f32[3,900]{1,0:T(4,128)} %copy-done.7, ...), custom_call_target="tpu_custom_call" | custom-call | tf_op jit(solution)/shard_map/operator/pallas_call | solution.py:387
  84.3 0.8 slice.9
  85.1 6.7 %collective-permute-start.5 = (f32[2,1000]{1,0:T(2,128)S(1)}, f32[2,1000]{1,0:T(2,128)S(1)}, u32[]{:S(2)}, u32[]{:S(2)}) collective-permute-start(f32[2,1000]{1,0:T(2,128)S(1)} %slice.9), channel_id=1, source_target_pairs={{4,0},{8,4},{12,8},{16,12},{20,16},{24,20},{28,24},{32,28},{36,32}... | collective-permute-start | bytes 24008 | tf_op jit(solution)/shard_map/ppermute | solution.py:430
  91.8 0.8 collective-permute-done.5
  92.6 1.2 %multiply_add_fusion = f32[1000,4]{1,0:T(8,128)S(1)} fusion(f32[1000,4]{1,0:T(8,128)} %get-tuple-element.14, f32[4]{0:T(128)S(1)} %compare_convert_fusion, f32[1000]{0:T(1024)S(1)} %bitcast.8), kind=kLoop, calls=%fused_computation | loop fusion | flops 8000 | bytes 36016 | tf_op jit(solution)/shard_map/add | solution.py:437
  93.8 0.8 copy.22
  94.6 0.2 copy-done
  94.9 0.2 multiply_add_fusion.1
  95.1 0.8 copy.21
  (30 shorter events, 0.1 us)
Async XLA Ops:
  0.6 8.6 %copy-start.3 = (f32[3,3,3,10,10]{4,2,3,1,0:T(4,128)S(1)}, f32[3,3,3,10,10]{4,2,3,1,0:T(4,128)}, u32[]{:S(2)}) copy-start(f32[3,3,3,10,10]{4,2,3,1,0:T(4,128)} %param.11) | copy-start | bytes 32404
  3.2 17.6 %collective-permute-start = (f32[504,128]{1,0:T(8,128)}, f32[504,128]{1,0:T(8,128)S(1)}, u32[]{:S(2)}, u32[]{:S(2)}) collective-permute-start(f32[504,128]{1,0:T(8,128)} %get-tuple-element.9), channel_id=1, source_target_pairs={{0,4},{4,8},{8,12},{12,16},{16,20},{20,24},{24,28},{28,32},{32,36}... | collective-permute-start | bytes 774152 | tf_op jit(solution)/shard_map/ppermute | solution.py:424
  7.3 13.6 %collective-permute-start.1 = (f32[504,128]{1,0:T(8,128)}, f32[504,128]{1,0:T(8,128)S(1)}, u32[]{:S(2)}, u32[]{:S(2)}) collective-permute-start(f32[504,128]{1,0:T(8,128)} %get-tuple-element.10), channel_id=1, source_target_pairs={{4,0},{8,4},{12,8},{16,12},{20,16},{24,20},{28,24},{32,28},{36,32}... | collective-permute-start | bytes 774152 | tf_op jit(solution)/shard_map/ppermute | solution.py:425
  9.3 5.1 %copy-start.13 = (s32[32]{0:T(128)S(1)}, s32[32]{0:T(128)}, u32[]{:S(2)}) copy-start(s32[32]{0:T(128)} %param.16) | copy-start | bytes 388
  9.4 7.5 %copy-start.4 = (f32[3,900]{1,0:T(4,128)}, f32[3,900]{1,0:T(4,128)S(1)}, u32[]{:S(2)}) copy-start(f32[3,900]{1,0:T(4,128)S(1)} %reshape.23.op0_ref) | copy-start | bytes 32404
  9.4 6.9 %copy-start.9 = (f32[2,10,10]{2,0,1:T(2,128)S(1)}, f32[2,10,10]{2,0,1:T(2,128)}, u32[]{:S(2)}) copy-start(f32[2,10,10]{2,0,1:T(2,128)} %param.12) | copy-start | bytes 2404
  9.5 11.4 %collective-permute-start.2 = (f32[3,900]{1,0:T(4,128)S(1)}, f32[3,900]{1,0:T(4,128)S(1)}, u32[]{:S(2)}, u32[]{:S(2)}) collective-permute-start(f32[3,900]{1,0:T(4,128)S(1)} %reshape.23.op0_ref), channel_id=1, source_target_pairs={{0,1},{1,2},{2,3},{3,0},{4,5},{5,6},{6,7},{7,4},{8,9},{9,10},{10,1... | collective-permute-start | bytes 32408 | tf_op jit(solution)/shard_map/ppermute | solution.py:420
  10.7 10.1 %collective-permute-start.3 = (f32[3,900]{1,0:T(4,128)S(1)}, f32[3,900]{1,0:T(4,128)S(1)}, u32[]{:S(2)}, u32[]{:S(2)}) collective-permute-start(f32[3,900]{1,0:T(4,128)S(1)} %reshape.23.op0_ref), channel_id=1, source_target_pairs={{0,2},{1,3},{2,0},{3,1},{4,6},{5,7},{6,4},{7,5},{8,10},{9,11},{10,... | collective-permute-start | bytes 32408 | tf_op jit(solution)/shard_map/ppermute | solution.py:420
  13.2 7.6 %collective-permute-start.4 = (f32[3,900]{1,0:T(4,128)S(1)}, f32[3,900]{1,0:T(4,128)S(1)}, u32[]{:S(2)}, u32[]{:S(2)}) collective-permute-start(f32[3,900]{1,0:T(4,128)S(1)} %reshape.23.op0_ref), channel_id=1, source_target_pairs={{0,3},{1,0},{2,1},{3,2},{4,7},{5,4},{6,5},{7,6},{8,11},{9,8},{10,9... | collective-permute-start | bytes 32408 | tf_op jit(solution)/shard_map/ppermute | solution.py:420
  15.7 0.7 copy-start.14
  16.9 0.7 copy-start.10
  17.6 1.3 %copy-start.12 = (s32[256]{0:T(256)S(1)}, s32[256]{0:T(256)}, u32[]{:S(2)}) copy-start(s32[256]{0:T(256)} %param.18) | copy-start | bytes 3076
  18.9 0.7 copy-start.5
  18.9 0.7 copy-start.11
  20.8 0.6 copy-start.6
  20.8 0.6 copy-start.7
  20.8 0.6 copy-start.8
  20.9 0.7 copy-start.1
  21.6 0.7 copy-start.2
  85.1 7.5 %collective-permute-start.5 = (f32[2,1000]{1,0:T(2,128)S(1)}, f32[2,1000]{1,0:T(2,128)S(1)}, u32[]{:S(2)}, u32[]{:S(2)}) collective-permute-start(f32[2,1000]{1,0:T(2,128)S(1)} %slice.9), channel_id=1, source_target_pairs={{4,0},{8,4},{12,8},{16,12},{20,16},{24,20},{28,24},{32,28},{36,32}... | collective-permute-start | bytes 24008 | tf_op jit(solution)/shard_map/ppermute | solution.py:430
  93.8 1.0 %copy-start = (f32[1000,32]{1,0:T(8,128)S(1)}, f32[1000,32]{1,0:T(8,128)}, u32[]{:S(2)}) copy-start(f32[1000,32]{1,0:T(8,128)} %get-tuple-element.12) | copy-start | bytes 384004
where the time goes:
time: 97.1 us; the launch traced here: 95.9 us
  Pallas kernels  64.6 us (67%)
  starting transfers between devices  17.6 us (18%)
  local copies, waits for them, and re-layouts  7.99 us (8%)
  other arithmetic  2.7 us (3%)
  between operations  2.17 us (2%)
    pallas_call x1, Pallas kernels, operator_step(): pl.pallas_call(main_kernel, out_shape=(shape((KKK, CAP)), shape((KKK, 32)...  62.1 us
    ppermute x1, starting transfers between devices, per_device(): lax.ppermute(sent[:2], 'box', [(i + 1, i) for i in range(count - 1)])  6.69 us
    unnamed x34, local copies, waits for them, and re-layouts  5.85 us
    ppermute x3, starting transfers between devices, per_device(): lax.ppermute(terms, 'rank', [(i, (i + step) % 4) for i in range(4)])  4.89 us
    ppermute x1, starting transfers between devices, per_device(): lax.ppermute(tail, 'box', [(i, i + 1) for i in range(count - 1)])  4.09 us
    pallas_call x1, Pallas kernels, edges(): pl.pallas_call(edges_kernel, out_shape=(shape((HALF, LANES)), shape((HALF...  2.57 us
  transfers between devices with their start and end apart: 6, of which 1 were waited for; matrix products, arithmetic and copies ran while one was open for 3% of the time, Pallas kernels for 0%

commit v1 on v0

v1 whole, which is shorter than its diff:
```python
import jax
import jax.numpy as jnp
import numpy as np
from jax import lax
from jax.experimental import pallas as pl
from jax.experimental.pallas import tpu as pltpu
from jax.sharding import PartitionSpec as P

F32 = jnp.float32
BF16 = jnp.bfloat16
I32 = jnp.int32
HIGHEST_MODE = lax.Precision.HIGHEST
CHILD_SCALE = 8.0 ** (-0.5)

K = 10
SQ = 100
KKK = 1000
CAP = 256
EDGE = 64
HALF = 504
LANES = 128
KT = 60
MROWS = 1008
GROUPS = 6

SAME_X = (0, 3, 4, 5, 6)
Y_CODE = {0: 0, 3: 1, 4: 2, 5: 0, 6: 0}
Z_CODE = {0: 0, 3: 0, 4: 0, 5: 1, 6: 2}


def split(value):
    high = value.astype(BF16)
    low = (value - high.astype(F32)).astype(BF16)
    return high, low


def mm(a, b):
    return jnp.dot(a, b, preferred_element_type=F32)


def mm_t(a, b):
    return lax.dot_general(a, b, (((1,), (1,)), ((), ())), preferred_element_type=F32)


def mm_full(a, b):
    return jnp.dot(a, b, preferred_element_type=F32, precision=HIGHEST_MODE)


def iota(shape, dim):
    return lax.broadcasted_iota(I32, shape, dim)


def tenth(index):
    return jnp.floor((index.astype(F32) + 0.5) * 0.1).astype(I32)


def edges_kernel(x_ref, nb_ref, head_ref, tail_ref):
    count = jnp.sum((nb_ref[0:1, :] >= 0).astype(F32), axis=1, keepdims=True)
    row = iota((2 * CAP, 2 * LANES), 0)
    lane = iota((2 * CAP, 2 * LANES), 1)
    slot = row & (CAP - 1)
    same_half = (row >= CAP) == ((lane & (LANES - 1)) >= EDGE)
    column = lane & (EDGE - 1)
    wanted = jnp.where(lane < LANES, column, column - EDGE + count.astype(I32))
    pick = ((slot == wanted) & same_half).astype(F32).astype(BF16)
    top_high, top_low = split(x_ref[0:HALF, :])
    below = jnp.concatenate([x_ref[HALF:KKK, :], jnp.zeros((2 * HALF - KKK, CAP), F32)], axis=0)
    low_high, low_low = split(below)
    both = mm(top_high, pick[:CAP]) + mm(top_low, pick[:CAP])
    both = both + (mm(low_high, pick[CAP:]) + mm(low_low, pick[CAP:]))
    head_ref[...] = both[:, :LANES]
    spot = (iota((HALF, LANES), 0) == HALF - 1) & (iota((HALF, LANES), 1) >= EDGE)
    tail_ref[...] = jnp.where(spot, count, both[:, LANES:])


def compress(value_ref, select, ff_high, ff_low, filter_smem, work_ref, out_ref):
    high, low = split(value_ref[0:KKK, :])
    span = KKK + 32
    grouped = mm_t(high, select) + mm_t(low, select)
    for w in range(4):
        work_ref[w * span : w * span + KKK, :] = grouped[:, w * LANES : (w + 1) * LANES]
        work_ref[w * span + KKK : (w + 1) * span, :] = jnp.zeros((32, LANES), F32)
    base = 4 * span
    for pair in range(5):
        columns = []
        for i in (2 * pair, 2 * pair + 1):
            columns.append(
                jnp.concatenate(
                    [work_ref[w * span + i * SQ : w * span + i * SQ + LANES, :] for w in range(4)],
                    axis=0,
                )
            )
        rhs_high, rhs_low = split(jnp.concatenate(columns, axis=1))
        z = mm(ff_high, rhs_high) + mm(ff_low, rhs_high) + mm(ff_high, rhs_low)
        work_ref[base + 208 * pair : base + 208 * pair + 104, :] = z[:, :LANES]
        work_ref[base + 208 * pair + 104 : base + 208 * pair + 208, :] = z[:, LANES:]
    upper = iota((1, LANES), 1) >= 64
    for a in range(K):
        total = None
        for i in range(K):
            weight = jnp.where(upper, filter_smem[a, 1, i], filter_smem[a, 0, i]) * CHILD_SCALE
            term = work_ref[base + 104 * i : base + 104 * i + 104, :] * weight
            total = term if total is None else total + term
        total = total + pltpu.roll(total, 64, axis=1)
        out_ref[a * SQ : (a + 1) * SQ, :] = total[:SQ]


def turned(value_ref, rows):
    high, low = split(value_ref[0:KKK, :])
    same = (iota((rows, LANES), 0) == iota((rows, LANES), 1)).astype(F32).astype(BF16)
    return mm_t(same, high) + mm_t(same, low)


def main_kernel(
    x_ref,
    left_ref,
    right_ref,
    op0_ref,
    op1_ref,
    op2_ref,
    op3_ref,
    near_ref,
    parent_one_ref,
    octant_one_ref,
    keep_ref,
    parent_two_ref,
    octant_two_ref,
    cols_ref,
    filter_ref,
    filter_smem,
    leaves_ref,
    one_ref,
    two_ref,
    send_ref,
    w_high,
    w_low,
    work,
    s_high,
    s_low,
    edge,
    b_wide,
    c_wide,
    ops,
    acc_ref,
    applied,
    level,
    level_up,
):
    ops[...] = jnp.zeros_like(ops)
    for n, ref in enumerate((op0_ref, op1_ref, op2_ref, op3_ref)):
        ops[3 * n : 3 * n + 3, 0:900] = ref[...]
    factors = ops[...]
    row = iota((104, LANES), 0)
    lane = iota((104, LANES), 1)
    spread = jnp.where(row < 80, (row >> 3) * 10 + (row & 7), 0)
    spread = jnp.where((row >= 80) & (row < 88), (row - 80) * 10 + 8, spread)
    spread = jnp.where((row >= 88) & (row < 96), (row - 88) * 10 + 9, spread)
    spread = jnp.where(row >= 96, 80 + ((row - 96) >> 1) * 10 + 8 + (row & 1), spread)
    order = ((spread == lane) & (row < 100)).astype(F32).astype(BF16)
    x_factor = []
    for code in range(3):
        moved = factors if code == 0 else pltpu.roll(factors, 1024 - SQ * code, axis=1)
        high, low = split(moved[:, :LANES])
        x_factor.append(mm_t(order, jnp.concatenate([high, low, high], axis=0)).astype(BF16))
    x_same = x_factor[0]
    x_moved = jnp.concatenate([x_factor[1], x_factor[2]], axis=0)
    column_of = iota((CAP, 512), 0)
    for wide_ref, axis in ((b_wide, 1), (c_wide, 2)):
        cols = (column_of == cols_ref[axis - 1 : axis, :]).astype(F32).astype(BF16)
        rows = [
            pltpu.roll(factors, 1024 - 300 * axis - 10 * b, axis=1)[:, :CAP] for b in range(K)
        ]
        high, low = split(jnp.concatenate(rows, axis=0))
        wide_ref[...] = (mm(high, cols) + mm(low, cols)).reshape(K, 16, 512)

    first_half = iota((HALF, LANES), 1) < EDGE
    left = left_ref[...]
    right = right_ref[...]
    edge[0:HALF, :] = jnp.where(first_half, left, pltpu.roll(right, EDGE, axis=1))
    edge[HALF : 2 * HALF, :] = jnp.where(first_half, pltpu.roll(left, EDGE, axis=1), right)
    near = near_ref[...]
    origin = near[0:1, 0:1]
    before = left[HALF - 1 : HALF, EDGE : EDGE + 1].astype(I32)
    moved = near - origin
    place = jnp.where(moved < 0, moved + (2 * CAP + EDGE) - before, moved)
    place = jnp.where(moved >= CAP, moved + EDGE, place)
    place = jnp.where(near >= 0, place, -1)
    live = (near[0:1, :] >= 0).astype(F32)
    slots = iota((CAP + LANES, CAP), 0)
    own_high, own_low = split(x_ref[...])
    far_high, far_low = split(edge[0:KKK, :])
    wide = jnp.concatenate([own_high, own_low, far_high, far_low], axis=1)
    half = KT * LANES
    for i in range(K):
        for h in range(2):
            at = h * half + i * 768
            work[at + 500 : at + 512, :] = jnp.zeros((12, LANES), F32)
            work[at + 612 : at + 640, :] = jnp.zeros((28, LANES), F32)
            work[at + 740 : at + 768, :] = jnp.zeros((28, LANES), F32)
    for e in range(7):
        if e == 0:
            taken = x_ref[...] * live
        else:
            pick = (slots == place[e : e + 1, :]).astype(F32).astype(BF16)
            taken = mm(
                wide,
                jnp.concatenate([pick[:CAP], pick[:CAP], pick[CAP:], pick[CAP:]], axis=0),
            )
        start = 0 if e == 0 else 512 if e == 1 else 640 if e == 2 else SQ * (e - 2)
        for h in range(2):
            hold = level if h == 0 else level_up
            hold[...] = taken[:, h * LANES : (h + 1) * LANES]
            for i in range(K):
                at = h * half + i * 768 + start
                work[at : at + SQ, :] = hold[i * SQ : (i + 1) * SQ, :]
    for h in range(2):
        for t in range(15):
            high, low = split(work[h * half + 512 * t : h * half + 512 * (t + 1), :])
            s_high[h, 512 * t : 512 * (t + 1), :] = high
            s_low[h, 512 * t : 512 * (t + 1), :] = low

    def build(pair_of, count, step, width):
        apart = 6 * width + 1

        def put(value, first_tile, position, tiles):
            for l in range(tiles):
                at = (first_tile + l) * width + position
                part = value[:, l * LANES : (l + 1) * LANES]
                for a in range(K):
                    work[pl.ds(at + a * step, 8, stride=apart), :] = part[8 * a : 8 * a + 8]
                for n, i in enumerate((8, 9)):
                    work[pl.ds(at + i * apart, 8, stride=step), :] = part[80 + 8 * n : 88 + 8 * n]
                for n, a in enumerate((8, 9)):
                    work[pl.ds(at + 8 * apart + a * step, 2, stride=apart), :] = part[
                        96 + 2 * n : 98 + 2 * n
                    ]

        held = []
        for u in range(count):
            b, c = pair_of(u)
            high, low = split(b_wide[b] * c_wide[c])
            rhs = jnp.concatenate([high, high, low], axis=0)
            for part in range(2):
                put(mm(x_same, rhs[:, 256 * part : 256 * part + 256]), 2 * part, u, 2)
            held.append(rhs[:, :LANES])
            if len(held) == 2:
                both = mm(x_moved, jnp.concatenate(held, axis=1))
                for n in range(2):
                    put(both[:104, n * LANES : (n + 1) * LANES], 4, u - 1 + n, 1)
                    put(both[104:, n * LANES : (n + 1) * LANES], 5, u - 1 + n, 1)
                held = []

    def one_group(g, carry):
        def pair_of(u):
            p = g * 16 + u
            b = (p * 205) >> 11
            return b, p - 10 * b

        build(pair_of, 16, 17, 170)
        first = pl.multiple_of(g * 160, 160)
        for t in range(KT):
            at = (t // 6) * 1021 + (t % 6) * 170
            for a in range(K):
                high, low = split(work[at + 17 * a : at + 17 * a + 16, :])
                w_high[t, pl.ds(first + 16 * a, 16), :] = high
                w_low[t, pl.ds(first + 16 * a, 16), :] = low
        return carry

    lax.fori_loop(0, GROUPS, one_group, 0)
    build(lambda u: (9, 6 + u), 4, 4, 48)
    for t in range(KT):
        at = (t // 6) * 289 + (t % 6) * 48
        high, low = split(work[at : at + 48, :])
        w_high[t, 960:MROWS, :] = high
        w_low[t, 960:MROWS, :] = low

    wide_high = jnp.concatenate([w_high[t] for t in range(KT)], axis=1)
    wide_low = jnp.concatenate([w_low[t] for t in range(KT)], axis=1)
    tall_high = jnp.concatenate([s_high[0], s_high[1]], axis=1)
    tall_low = jnp.concatenate([s_low[0], s_low[1]], axis=1)
    acc_ref[...] = mm(wide_high, tall_high)
    acc_ref[...] += mm(wide_low, tall_high)
    acc_ref[...] += mm(wide_high, tall_low)
    for a in range(K):
        for g in range(GROUPS):
            applied[a * SQ + 16 * g : a * SQ + 16 * g + 16, :] = acc_ref[
                g * 160 + a * 16 : g * 160 + a * 16 + 16, :
            ]
        applied[a * SQ + 96 : a * SQ + SQ, :] = acc_ref[960 + 4 * a : 964 + 4 * a, :]
    leaves_ref[...] = applied[...] * keep_ref[...].astype(F32)

    p_row = iota((104, 16), 0)
    small = iota((104, 16), 1)
    b_of = tenth(p_row)
    c_of = p_row - 10 * b_of
    pick_b = ((b_of == small) & (p_row < SQ)).astype(F32).astype(BF16)
    pick_c = ((c_of == small) & (p_row < SQ)).astype(F32).astype(BF16)
    q_lane = iota((LANES, LANES), 1)
    j_of = tenth(q_lane)
    k_of = q_lane - 10 * j_of
    small = iota((LANES, LANES), 0)
    pick_j = ((j_of == small) & (q_lane < SQ)).astype(F32).astype(BF16)
    pick_k = ((k_of == small) & (q_lane < SQ)).astype(F32).astype(BF16)
    ops[...] = jnp.zeros_like(ops)
    for f in range(2):
        ops[0:K, f * LANES : f * LANES + K] = filter_ref[:, f, :]
    high, low = split(ops[:, 0 : 2 * LANES])
    square = jnp.concatenate([high, low], axis=1)

    def spread_filter(pick_row, pick_lane):
        grown = mm(pick_row, square).astype(BF16)
        parts = [mm(grown[:, n * LANES : (n + 1) * LANES], pick_lane) for n in range(4)]
        return parts[0] + parts[2], parts[1] + parts[3]

    y_filter = spread_filter(pick_b, pick_j)
    z_filter = spread_filter(pick_c, pick_k)
    ff = jnp.concatenate(
        [y_filter[0] * z_filter[0], y_filter[1] * z_filter[0], y_filter[0] * z_filter[1], y_filter[1] * z_filter[1]],
        axis=1,
    )
    ff_high, ff_low = split(ff)
    parent = parent_one_ref[...]
    octant = octant_one_ref[...]
    local = parent - (origin >> 3)
    local = jnp.where(local < 0, 32, local)
    code = (octant >> 1) * LANES + (octant & 1) * 64 + local
    code = jnp.where(parent >= 0, code, -1)
    rows = iota((4 * LANES, CAP), 0)
    select = (rows == code).astype(F32).astype(BF16)
    compress(applied, select, ff_high, ff_low, filter_smem, work, level)
    parent = parent_two_ref[...]
    octant = octant_two_ref[...]
    local = parent - (origin >> 6)
    local = jnp.where(local < 0, 4, local)
    code = (octant >> 1) * LANES + (octant & 1) * 64 + local
    code = jnp.where(parent >= 0, code, -1)
    last = (octant[:, 0:1] + 7) & 7
    last = (last >> 1) * LANES + (last & 1) * 64 + 4
    code = jnp.concatenate([code, jnp.broadcast_to(last, (1, 32)), jnp.full((1, 64), -1, I32)], axis=1)
    rows = iota((4 * LANES, LANES), 0)
    lane = iota((4 * LANES, LANES), 1)
    select = ((rows == code) & (lane <= 32)).astype(F32).astype(BF16)
    compress(level, select, ff_high, ff_low, filter_smem, work, level_up)
    one = turned(level, 40)
    two = turned(level_up, 8)
    one_ref[...] = one[:32]
    two_ref[...] = two[:4]
    send_ref[0:1, :] = one[32:33]
    send_ref[1:2, :] = two[4:5]


def finish_kernel(one_ref, two_ref, in_ref, parent_one_ref, parent_two_ref, one_out, two_out):
    for ref, parent_ref, out, n in ((one_ref, parent_one_ref, one_out, 0), (two_ref, parent_two_ref, two_out, 1)):
        rows = ref.shape[0]
        last = jnp.max(parent_ref[...], axis=1, keepdims=True) & (rows - 1)
        mask = (iota((rows, 1), 0) == last).astype(F32)
        out[...] = ref[...] + mask * in_ref[n : n + 1, :]


def column_table():
    table = np.full((8, 512), -1, np.int32)
    for n, e in enumerate(SAME_X):
        for j in range(K):
            for k in range(K):
                at = n * SQ + j * K + k
                table[0, at] = Y_CODE[e] * SQ + j
                table[1, at] = Z_CODE[e] * SQ + k
    return table


VMEM_SPEC = pl.BlockSpec(memory_space=pltpu.VMEM)
SMEM_SPEC = pl.BlockSpec(memory_space=pltpu.SMEM)
PARAMS = pltpu.CompilerParams(vmem_limit_bytes=63 * 1024 * 1024)


def shape(dims, dtype=F32):
    return jax.ShapeDtypeStruct(dims, dtype)


def edges(coeffs, neighbours):
    return pl.pallas_call(
        edges_kernel,
        out_shape=(shape((HALF, LANES)), shape((HALF, LANES))),
        in_specs=[VMEM_SPEC] * 2,
        out_specs=(VMEM_SPEC,) * 2,
        name="edges",
    )(coeffs, neighbours)


def operator_step(coeffs, from_left, from_right, terms, ints, filters):
    turned_filters = jnp.transpose(filters, (1, 0, 2))
    return pl.pallas_call(
        main_kernel,
        out_shape=(shape((KKK, CAP)), shape((32, KKK)), shape((4, KKK)), shape((2, KKK))),
        in_specs=[VMEM_SPEC] * 15 + [SMEM_SPEC],
        out_specs=(VMEM_SPEC,) * 4,
        scratch_shapes=[
            pltpu.VMEM((KT, MROWS, LANES), BF16),
            pltpu.VMEM((KT, MROWS, LANES), BF16),
            pltpu.VMEM((2 * KT * LANES, LANES), F32),
            pltpu.VMEM((2, KT * LANES, LANES), BF16),
            pltpu.VMEM((2, KT * LANES, LANES), BF16),
            pltpu.VMEM((2 * HALF, LANES), F32),
            pltpu.VMEM((K, 16, 512), F32),
            pltpu.VMEM((K, 16, 512), F32),
            pltpu.VMEM((16, 1024), F32),
            pltpu.VMEM((MROWS, CAP), F32),
            pltpu.VMEM((KKK, CAP), F32),
            pltpu.VMEM((KKK, LANES), F32),
            pltpu.VMEM((KKK, LANES), F32),
        ],
        compiler_params=PARAMS,
        name="operator",
    )(
        coeffs,
        from_left,
        from_right,
        *terms,
        *ints,
        jnp.asarray(column_table()),
        turned_filters,
        turned_filters,
    )


def finish(one, two, received, parent_one, parent_two):
    return pl.pallas_call(
        finish_kernel,
        out_shape=(shape((32, KKK)), shape((4, KKK))),
        in_specs=[VMEM_SPEC] * 5,
        out_specs=(VMEM_SPEC,) * 2,
        name="finish",
    )(one, two, received, parent_one, parent_two)


def per_device(
    coeffs, operator, filters, neighbours, parent_one, octant_one, parent_two, octant_two, keep
):
    terms = operator.reshape(3, 900)
    others = [
        lax.ppermute(terms, "rank", [(i, (i + step) % 4) for i in range(4)]) for step in (1, 2, 3)
    ]
    head, tail = edges(coeffs, neighbours)
    count = lax.axis_size("box")
    from_left = lax.ppermute(tail, "box", [(i, i + 1) for i in range(count - 1)])
    from_right = lax.ppermute(head, "box", [(i + 1, i) for i in range(count - 1)])
    rows = [v[None] for v in (parent_one, octant_one, keep, parent_two, octant_two)]
    leaves, one, two, sent = operator_step(
        coeffs, from_left, from_right, (terms, *others), (neighbours, *rows), filters
    )
    received = lax.ppermute(sent, "box", [(i + 1, i) for i in range(count - 1)])
    one, two = finish(one, two, received, rows[0], rows[3])
    return leaves, one.T, two.T


def solution(mesh):
    placed = (
        P(None, "box"),
        P("rank", None, None, None, None),
        P(),
        P(None, "box"),
        P("box"),
        P("box"),
        P("box"),
        P("box"),
        P("box"),
    )
    return jax.shard_map(
        per_device,
        mesh=mesh,
        in_specs=placed,
        out_specs=(P(None, "box"), P(None, "box"), P(None, "box")),
        check_vma=False,
    )
```

time: 97.1 us -> 64.3 us (0.66)
  Pallas kernels: 64.6 us -> 39.6 us
  local copies, waits for them, and re-layouts: 7.99 us -> 1.52 us
  waiting for transfers between devices: 0.8 us -> 4.21 us
  other arithmetic: 2.7 us -> 0 us
  between operations: 2.17 us -> 0.73 us
    pallas_call x1 -> x2, Pallas kernels: 62.1 us -> 37 us  [the longest x1 35.3 us: operator_step(): pl.pallas_call(main_kernel, out_shape=(shape((KKK, CAP)), shape((32, KKK)...]
    unnamed x34 -> x17, local copies, waits for them, and re-layouts: 5.85 us -> 1.38 us
    ppermute x3, waiting for transfers between devices: 0.01 us -> 3.19 us  [per_device(): lax.ppermute(terms, 'rank', [(i, (i + step) % 4) for i in range(4)])]
    add x2 -> x0, other arithmetic: 1.43 us -> none  [the longest x1 1.23 us: per_device(): level_two + received[1][:, None] * (slots_two == last_two)[None, :].astyp...]
    reduce_max x2 -> x0, other arithmetic: 1.26 us -> none  [the longest x1 0.63 us: per_device(): last_two = jnp.max(parent_two) - me * level_two.shape[1]]
    concatenate x2 -> x0, local copies, waits for them, and re-layouts: 1.23 us -> none  [gather_ints(): return jnp.concatenate(rows, axis=0)]
    ppermute x3, starting transfers between devices: 4.89 us -> 3.68 us  [per_device(): lax.ppermute(terms, 'rank', [(i, (i + step) % 4) for i in range(4)])]
  transfers between devices with their start and end apart: 6 -> 6, of which waited for: 1 -> 3; matrix products, arithmetic and copies ran while one was open for 3% -> 0% of each run, Pallas kernels for 0% -> 0%
where the time goes in v1:
time: 64.3 us; the launch traced here: 63.3 us
  Pallas kernels  39.6 us (62%)
  starting transfers between devices  17.2 us (27%)
  waiting for transfers between devices  4.21 us (7%)
  local copies, waits for them, and re-layouts  1.52 us (2%)
  between operations  0.73 us (1%)
    pallas_call x1, Pallas kernels, operator_step(): pl.pallas_call(main_kernel, out_shape=(shape((KKK, CAP)), shape((32, KKK)...  35.3 us
    ppermute x1, starting transfers between devices, per_device(): received = lax.ppermute(sent, 'box', [(i + 1, i) for i in range(count - 1)])  7.55 us
    ppermute x1, starting transfers between devices, per_device(): lax.ppermute(tail, 'box', [(i, i + 1) for i in range(count - 1)])  4.09 us
    ppermute x3, starting transfers between devices, per_device(): lax.ppermute(terms, 'rank', [(i, (i + step) % 4) for i in range(4)])  3.68 us
    ppermute x3, waiting for transfers between devices, per_device(): lax.ppermute(terms, 'rank', [(i, (i + step) % 4) for i in range(4)])  3.19 us
    pallas_call x1, Pallas kernels, edges(): pl.pallas_call(edges_kernel, out_shape=(shape((HALF, LANES)), shape((HALF...  2.57 us
    ppermute x1, starting transfers between devices, per_device(): lax.ppermute(head, 'box', [(i + 1, i) for i in range(count - 1)])  1.92 us
    pallas_call x1, Pallas kernels, finish(): pl.pallas_call(finish_kernel, out_shape=(shape((32, KKK)), shape((4, KKK)...  1.78 us
  transfers between devices with their start and end apart: 6, of which 3 were waited for; matrix products, arithmetic and copies ran while one was open for 0% of the time, Pallas kernels for 0%

profile of v1, /device:TPU:25, one launch (start us, length us, event | category | flops | bytes accessed | tf_op | source)
XLA Modules:
  0.0 63.3 jit_solution(16502597723884865823)
XLA Ops:
  0.6 0.0 copy-start.2
  0.6 2.6 %edges.1 = (f32[504,128]{1,0:T(8,128)}, f32[504,128]{1,0:T(8,128)}) custom-call(f32[1000,256]{1,0:T(8,128)} %x_ref.3, s32[7,256]{1,0:T(8,128)} %near_ref.1), custom_call_target="tpu_custom_call" | custom-call | tf_op jit(solution)/shard_map/edges/pallas_call | solution.py:381
  3.2 4.1 %collective-permute-start = (f32[504,128]{1,0:T(8,128)}, f32[504,128]{1,0:T(8,128)S(1)}, u32[]{:S(2)}, u32[]{:S(2)}) collective-permute-start(f32[504,128]{1,0:T(8,128)} %get-tuple-element.11), channel_id=1, source_target_pairs={{0,4},{4,8},{8,12},{12,16},{16,20},{20,24},{24,28},{28,32},{32,36}... | collective-permute-start | bytes 774152 | tf_op jit(solution)/shard_map/ppermute | solution.py:445
  7.3 1.9 %collective-permute-start.1 = (f32[504,128]{1,0:T(8,128)}, f32[504,128]{1,0:T(8,128)S(1)}, u32[]{:S(2)}, u32[]{:S(2)}) collective-permute-start(f32[504,128]{1,0:T(8,128)} %get-tuple-element.12), channel_id=1, source_target_pairs={{4,0},{8,4},{12,8},{16,12},{20,16},{24,20},{28,24},{32,28},{36,32}... | collective-permute-start | bytes 774152 | tf_op jit(solution)/shard_map/ppermute | solution.py:446
  9.2 0.0 copy-done.2
  9.3 0.1 reshape.9.op0_ref
  9.4 0.0 copy-start.3
  9.4 2.6 %collective-permute-start.4 = (f32[3,900]{1,0:T(4,128)S(1)}, f32[3,900]{1,0:T(4,128)S(1)}, u32[]{:S(2)}, u32[]{:S(2)}) collective-permute-start(f32[3,900]{1,0:T(4,128)S(1)} %reshape.9.op0_ref), channel_id=1, source_target_pairs={{0,3},{1,0},{2,1},{3,2},{4,7},{5,4},{6,5},{7,6},{8,11},{9,8},{10,9... | collective-permute-start | bytes 32408 | tf_op jit(solution)/shard_map/ppermute | solution.py:441
  12.0 0.5 collective-permute-start.3
  12.5 0.6 collective-permute-start.2
  13.1 0.0 collective-permute-done.4.op3_ref
  13.1 0.0 copy-start.4
  13.1 3.0 %collective-permute-done.3.op2_ref = f32[3,900]{1,0:T(4,128)S(1)} collective-permute-done((f32[3,900]{1,0:T(4,128)S(1)}, f32[3,900]{1,0:T(4,128)S(1)}, u32[]{:S(2)}, u32[]{:S(2)}) %collective-permute-start.3) | collective-permute-done | bytes 10832 | tf_op jit(solution)/shard_map/ppermute | solution.py:441
  16.1 0.0 copy-start.5
  16.1 0.2 collective-permute-done.2.op1_ref
  16.3 0.0 copy-start.6
  16.3 0.0 collective-permute-done.left_ref
  16.3 0.0 copy-start
  16.3 0.0 collective-permute-done.1.right_ref
  16.3 0.0 copy-start.1
  16.3 0.0 copy-done.3
  16.3 0.0 copy-done.4
  16.4 0.3 copy-done.5
  16.7 0.2 copy-done.6
  16.9 0.1 copy-done
  17.0 0.1 copy-done.1
  17.1 35.3 %operator.1 = (f32[1000,256]{1,0:T(8,128)}, f32[32,1000]{1,0:T(8,128)}, f32[4,1000]{1,0:T(4,128)}, f32[2,1000]{1,0:T(2,128)}) custom-call(f32[1000,256]{1,0:T(8,128)} %x_ref.3, f32[504,128]{1,0:T(8,128)} %copy-done, f32[504,128]{1,0:T(8,128)} %copy-done.1, f32[3,900]{1,0:T(4,128)} %copy-done.3, f32[3,900]{1,0:T(4,128)} %copy-done.6, f32[3,900]{1,0:T(4,128)} %copy-done.5, ...), custom_call_target="tpu_custom_call" | custom-call | tf_op jit(solution)/shard_map/operator/pallas_call | solution.py:392
  52.4 7.6 %collective-permute-start.5 = (f32[2,1000]{1,0:T(2,128)}, f32[2,1000]{1,0:T(2,128)S(1)}, u32[]{:S(2)}, u32[]{:S(2)}) collective-permute-start(f32[2,1000]{1,0:T(2,128)} %get-tuple-element.16), channel_id=1, source_target_pairs={{4,0},{8,4},{12,8},{16,12},{20,16},{24,20},{28,24},{32,28},{36,32}... | collective-permute-start | bytes 24008 | tf_op jit(solution)/shard_map/ppermute | solution.py:451
  59.9 1.0 %collective-permute-done.5.in_ref = f32[2,1000]{1,0:T(2,128)S(1)} collective-permute-done((f32[2,1000]{1,0:T(2,128)}, f32[2,1000]{1,0:T(2,128)S(1)}, u32[]{:S(2)}, u32[]{:S(2)}) %collective-permute-start.5) | collective-permute-done | bytes 8032 | tf_op jit(solution)/shard_map/ppermute | solution.py:451
  60.9 0.0 copy-start.7
  60.9 0.6 copy-done.7
  61.5 1.8 %finish.1 = (f32[32,1000]{1,0:T(8,128)}, f32[4,1000]{1,0:T(4,128)}) custom-call(f32[32,1000]{1,0:T(8,128)} %get-tuple-element.14.one_ref, f32[4,1000]{1,0:T(4,128)} %get-tuple-element.15.two_ref, f32[2,1000]{1,0:T(2,128)} %copy-done.7, s32[1,256]{1,0:T(1,128)} %bitcast.11, s32[1,32]{1,0:T(1,128)} %bitcast.13), custom_call_target="tpu_custom_call" | custom-call | tf_op jit(solution)/shard_map/finish/pallas_call | solution.py:427
  (1 shorter events, 0.0 us)
Async XLA Ops:
  0.6 8.6 %copy-start.2 = (f32[3,3,3,10,10]{4,2,3,1,0:T(4,128)S(1)}, f32[3,3,3,10,10]{4,2,3,1,0:T(4,128)}, u32[]{:S(2)}) copy-start(f32[3,3,3,10,10]{4,2,3,1,0:T(4,128)} %param.11) | copy-start | bytes 32404
  3.2 13.1 %collective-permute-start = (f32[504,128]{1,0:T(8,128)}, f32[504,128]{1,0:T(8,128)S(1)}, u32[]{:S(2)}, u32[]{:S(2)}) collective-permute-start(f32[504,128]{1,0:T(8,128)} %get-tuple-element.11), channel_id=1, source_target_pairs={{0,4},{4,8},{8,12},{12,16},{16,20},{20,24},{24,28},{28,32},{32,36}... | collective-permute-start | bytes 774152 | tf_op jit(solution)/shard_map/ppermute | solution.py:445
  7.3 9.0 %collective-permute-start.1 = (f32[504,128]{1,0:T(8,128)}, f32[504,128]{1,0:T(8,128)S(1)}, u32[]{:S(2)}, u32[]{:S(2)}) collective-permute-start(f32[504,128]{1,0:T(8,128)} %get-tuple-element.12), channel_id=1, source_target_pairs={{4,0},{8,4},{12,8},{16,12},{20,16},{24,20},{28,24},{32,28},{36,32}... | collective-permute-start | bytes 774152 | tf_op jit(solution)/shard_map/ppermute | solution.py:446
  9.4 6.9 %copy-start.3 = (f32[3,900]{1,0:T(4,128)}, f32[3,900]{1,0:T(4,128)S(1)}, u32[]{:S(2)}) copy-start(f32[3,900]{1,0:T(4,128)S(1)} %reshape.9.op0_ref) | copy-start | bytes 32404
  9.4 3.7 %collective-permute-start.4 = (f32[3,900]{1,0:T(4,128)S(1)}, f32[3,900]{1,0:T(4,128)S(1)}, u32[]{:S(2)}, u32[]{:S(2)}) collective-permute-start(f32[3,900]{1,0:T(4,128)S(1)} %reshape.9.op0_ref), channel_id=1, source_target_pairs={{0,3},{1,0},{2,1},{3,2},{4,7},{5,4},{6,5},{7,6},{8,11},{9,8},{10,9... | collective-permute-start | bytes 32408 | tf_op jit(solution)/shard_map/ppermute | solution.py:441
  12.0 4.1 %collective-permute-start.3 = (f32[3,900]{1,0:T(4,128)S(1)}, f32[3,900]{1,0:T(4,128)S(1)}, u32[]{:S(2)}, u32[]{:S(2)}) collective-permute-start(f32[3,900]{1,0:T(4,128)S(1)} %reshape.9.op0_ref), channel_id=1, source_target_pairs={{0,2},{1,3},{2,0},{3,1},{4,6},{5,7},{6,4},{7,5},{8,10},{9,11},{10,... | collective-permute-start | bytes 32408 | tf_op jit(solution)/shard_map/ppermute | solution.py:441
  12.5 3.8 %collective-permute-start.2 = (f32[3,900]{1,0:T(4,128)S(1)}, f32[3,900]{1,0:T(4,128)S(1)}, u32[]{:S(2)}, u32[]{:S(2)}) collective-permute-start(f32[3,900]{1,0:T(4,128)S(1)} %reshape.9.op0_ref), channel_id=1, source_target_pairs={{0,1},{1,2},{2,3},{3,0},{4,5},{5,6},{6,7},{7,4},{8,9},{9,10},{10,1... | collective-permute-start | bytes 32408 | tf_op jit(solution)/shard_map/ppermute | solution.py:441
  13.1 3.2 %copy-start.4 = (f32[3,900]{1,0:T(4,128)}, f32[3,900]{1,0:T(4,128)S(1)}, u32[]{:S(2)}) copy-start(f32[3,900]{1,0:T(4,128)S(1)} %collective-permute-done.4.op3_ref) | copy-start | bytes 32404
  16.1 0.6 copy-start.5
  16.3 0.6 copy-start.6
  16.3 0.7 %copy-start = (f32[504,128]{1,0:T(8,128)}, f32[504,128]{1,0:T(8,128)S(1)}, u32[]{:S(2)}) copy-start(f32[504,128]{1,0:T(8,128)S(1)} %collective-permute-done.left_ref) | copy-start | bytes 774148
  16.3 0.8 %copy-start.1 = (f32[504,128]{1,0:T(8,128)}, f32[504,128]{1,0:T(8,128)S(1)}, u32[]{:S(2)}) copy-start(f32[504,128]{1,0:T(8,128)S(1)} %collective-permute-done.1.right_ref) | copy-start | bytes 774148
  52.4 8.6 %collective-permute-start.5 = (f32[2,1000]{1,0:T(2,128)}, f32[2,1000]{1,0:T(2,128)S(1)}, u32[]{:S(2)}, u32[]{:S(2)}) collective-permute-start(f32[2,1000]{1,0:T(2,128)} %get-tuple-element.16), channel_id=1, source_target_pairs={{4,0},{8,4},{12,8},{16,12},{20,16},{24,20},{28,24},{32,28},{36,32}... | collective-permute-start | bytes 24008 | tf_op jit(solution)/shard_map/ppermute | solution.py:451
  60.9 0.6 copy-start.7

commit v2 on v1

--- a/solution.py
+++ b/solution.py
@@ -54,26 +54,28 @@
     return jnp.floor((index.astype(F32) + 0.5) * 0.1).astype(I32)
 
 
-def edges_kernel(x_ref, nb_ref, head_ref, tail_ref):
+def edges_kernel(x_ref, nb_ref, chip_ref, next_ref):
     count = jnp.sum((nb_ref[0:1, :] >= 0).astype(F32), axis=1, keepdims=True)
     row = iota((2 * CAP, 2 * LANES), 0)
     lane = iota((2 * CAP, 2 * LANES), 1)
     slot = row & (CAP - 1)
     same_half = (row >= CAP) == ((lane & (LANES - 1)) >= EDGE)
     column = lane & (EDGE - 1)
-    wanted = jnp.where(lane < LANES, column, column - EDGE + count.astype(I32))
+    odd = (nb_ref[0:1, 0:1] >> 8) & 1
+    from_head = (lane < LANES) == (odd == 1)
+    wanted = jnp.where(from_head, column, column - EDGE + count.astype(I32))
     pick = ((slot == wanted) & same_half).astype(F32).astype(BF16)
     top_high, top_low = split(x_ref[0:HALF, :])
     below = jnp.concatenate([x_ref[HALF:KKK, :], jnp.zeros((2 * HALF - KKK, CAP), F32)], axis=0)
     low_high, low_low = split(below)
     both = mm(top_high, pick[:CAP]) + mm(top_low, pick[:CAP])
     both = both + (mm(low_high, pick[CAP:]) + mm(low_low, pick[CAP:]))
-    head_ref[...] = both[:, :LANES]
     spot = (iota((HALF, LANES), 0) == HALF - 1) & (iota((HALF, LANES), 1) >= EDGE)
-    tail_ref[...] = jnp.where(spot, count, both[:, LANES:])
-
-
-def compress(value_ref, select, ff_high, ff_low, filter_smem, work_ref, out_ref):
+    chip_ref[...] = jnp.where(spot, count, both[:, :LANES])
+    next_ref[...] = jnp.where(spot, count, both[:, LANES:])
+
+
+def compress(value_ref, select, ff_both, filter_smem, work_ref, out_ref):
     high, low = split(value_ref[0:KKK, :])
     span = KKK + 32
     grouped = mm_t(high, select) + mm_t(low, select)
@@ -91,7 +93,8 @@
                 )
             )
         rhs_high, rhs_low = split(jnp.concatenate(columns, axis=1))
-        z = mm(ff_high, rhs_high) + mm(ff_low, rhs_high) + mm(ff_high, rhs_low)
+        z = mm(ff_both, rhs_high)
+        z = (z[:112] + z[112:] + mm(ff_both[:112], rhs_low))[:104]
         work_ref[base + 208 * pair : base + 208 * pair + 104, :] = z[:, :LANES]
         work_ref[base + 208 * pair + 104 : base + 208 * pair + 208, :] = z[:, LANES:]
     upper = iota((1, LANES), 1) >= 64
@@ -113,8 +116,8 @@
 
 def main_kernel(
     x_ref,
-    left_ref,
-    right_ref,
+    chip_ref,
+    next_ref,
     op0_ref,
     op1_ref,
     op2_ref,
@@ -135,14 +138,13 @@
     w_high,
     w_low,
     work,
+    spare,
     s_high,
     s_low,
     edge,
     b_wide,
     c_wide,
     ops,
-    acc_ref,
-    applied,
     level,
     level_up,
 ):
@@ -174,12 +176,13 @@
         wide_ref[...] = (mm(high, cols) + mm(low, cols)).reshape(K, 16, 512)
 
     first_half = iota((HALF, LANES), 1) < EDGE
-    left = left_ref[...]
-    right = right_ref[...]
+    near = near_ref[...]
+    origin = near[0:1, 0:1]
+    odd = ((origin >> 8) & 1) == 1
+    left = jnp.where(odd, chip_ref[...], next_ref[...])
+    right = jnp.where(odd, next_ref[...], chip_ref[...])
     edge[0:HALF, :] = jnp.where(first_half, left, pltpu.roll(right, EDGE, axis=1))
     edge[HALF : 2 * HALF, :] = jnp.where(first_half, pltpu.roll(left, EDGE, axis=1), right)
-    near = near_ref[...]
-    origin = near[0:1, 0:1]
     before = left[HALF - 1 : HALF, EDGE : EDGE + 1].astype(I32)
     moved = near - origin
     place = jnp.where(moved < 0, moved + (2 * CAP + EDGE) - before, moved)
@@ -208,18 +211,20 @@
             )
         start = 0 if e == 0 else 512 if e == 1 else 640 if e == 2 else SQ * (e - 2)
         for h in range(2):
-            hold = level if h == 0 else level_up
-            hold[...] = taken[:, h * LANES : (h + 1) * LANES]
+            part = taken[:, h * LANES : (h + 1) * LANES]
             for i in range(K):
                 at = h * half + i * 768 + start
-                work[at : at + SQ, :] = hold[i * SQ : (i + 1) * SQ, :]
+                lead = 4 * (i % 2)
+                if lead:
+                    work[at : at + 4, :] = part[i * SQ - 4 : i * SQ + 4][4:]
+                work[at + lead : at + SQ, :] = part[i * SQ + lead : (i + 1) * SQ]
     for h in range(2):
         for t in range(15):
             high, low = split(work[h * half + 512 * t : h * half + 512 * (t + 1), :])
             s_high[h, 512 * t : 512 * (t + 1), :] = high
             s_low[h, 512 * t : 512 * (t + 1), :] = low
 
-    def build(pair_of, count, step, width):
+    def build(stage, pair_of, count, step, width, between):
         apart = 6 * width + 1
 
         def put(value, first_tile, position, tiles):
@@ -227,11 +232,11 @@
                 at = (first_tile + l) * width + position
                 part = value[:, l * LANES : (l + 1) * LANES]
                 for a in range(K):
-                    work[pl.ds(at + a * step, 8, stride=apart), :] = part[8 * a : 8 * a + 8]
+                    stage[pl.ds(at + a * step, 8, stride=apart), :] = part[8 * a : 8 * a + 8]
                 for n, i in enumerate((8, 9)):
-                    work[pl.ds(at + i * apart, 8, stride=step), :] = part[80 + 8 * n : 88 + 8 * n]
+                    stage[pl.ds(at + i * apart, 8, stride=step), :] = part[80 + 8 * n : 88 + 8 * n]
                 for n, a in enumerate((8, 9)):
-                    work[pl.ds(at + 8 * apart + a * step, 2, stride=apart), :] = part[
+                    stage[pl.ds(at + 8 * apart + a * step, 2, stride=apart), :] = part[
                         96 + 2 * n : 98 + 2 * n
                     ]
 
@@ -249,48 +254,69 @@
                     put(both[:104, n * LANES : (n + 1) * LANES], 4, u - 1 + n, 1)
                     put(both[104:, n * LANES : (n + 1) * LANES], 5, u - 1 + n, 1)
                 held = []
-
-    def one_group(g, carry):
+            between(u)
+
+    def pair_in(g):
         def pair_of(u):
             p = g * 16 + u
             b = (p * 205) >> 11
             return b, p - 10 * b
 
-        build(pair_of, 16, 17, 170)
+        return pair_of
+
+    def convert(stage, g, count):
         first = pl.multiple_of(g * 160, 160)
-        for t in range(KT):
-            at = (t // 6) * 1021 + (t % 6) * 170
-            for a in range(K):
-                high, low = split(work[at + 17 * a : at + 17 * a + 16, :])
+
+        def between(u):
+            for unit in range(u * KT * K // count, (u + 1) * KT * K // count):
+                t, a = divmod(unit, K)
+                at = (t // 6) * 1021 + (t % 6) * 170 + 17 * a
+                high, low = split(stage[at : at + 16, :])
                 w_high[t, pl.ds(first + 16 * a, 16), :] = high
                 w_low[t, pl.ds(first + 16 * a, 16), :] = low
+
+        return between
+
+    def two_groups(n, carry):
+        g = 2 * n
+        ahead = jnp.where(n == 0, GROUPS - 1, g - 1)
+        build(work, pair_in(g), 16, 17, 170, convert(spare, ahead, 16))
+        build(spare, pair_in(g + 1), 16, 17, 170, convert(work, g, 16))
         return carry
 
-    lax.fori_loop(0, GROUPS, one_group, 0)
-    build(lambda u: (9, 6 + u), 4, 4, 48)
+    lax.fori_loop(0, GROUPS // 2, two_groups, 0)
+    build(work, lambda u: (9, 6 + u), 4, 4, 48, convert(spare, GROUPS - 1, 4))
     for t in range(KT):
         at = (t // 6) * 289 + (t % 6) * 48
         high, low = split(work[at : at + 48, :])
         w_high[t, 960:MROWS, :] = high
         w_low[t, 960:MROWS, :] = low
 
-    wide_high = jnp.concatenate([w_high[t] for t in range(KT)], axis=1)
-    wide_low = jnp.concatenate([w_low[t] for t in range(KT)], axis=1)
     tall_high = jnp.concatenate([s_high[0], s_high[1]], axis=1)
     tall_low = jnp.concatenate([s_low[0], s_low[1]], axis=1)
-    acc_ref[...] = mm(wide_high, tall_high)
-    acc_ref[...] += mm(wide_low, tall_high)
-    acc_ref[...] += mm(wide_high, tall_low)
-    for a in range(K):
-        for g in range(GROUPS):
-            applied[a * SQ + 16 * g : a * SQ + 16 * g + 16, :] = acc_ref[
-                g * 160 + a * 16 : g * 160 + a * 16 + 16, :
-            ]
-        applied[a * SQ + 96 : a * SQ + SQ, :] = acc_ref[960 + 4 * a : 964 + 4 * a, :]
-    leaves_ref[...] = applied[...] * keep_ref[...].astype(F32)
-
-    p_row = iota((104, 16), 0)
-    small = iota((104, 16), 1)
+    middle = KT // 2
+    first = [w_high[t] for t in range(KT)] + [w_low[t] for t in range(middle)]
+    second = [w_low[t] for t in range(middle, KT)] + [w_high[t] for t in range(KT)]
+    total = mm(
+        jnp.concatenate(first, axis=1),
+        jnp.concatenate([tall_high, tall_high[: middle * LANES]], axis=0),
+    ) + mm(
+        jnp.concatenate(second, axis=1),
+        jnp.concatenate([tall_high[middle * LANES :], tall_low], axis=0),
+    )
+    for h in range(2):
+        at = h * MROWS
+        columns = slice(h * LANES, (h + 1) * LANES)
+        spare[at : at + MROWS, :] = total[:, columns]
+        for a in range(K):
+            for g in range(GROUPS):
+                leaves_ref[a * SQ + 16 * g : a * SQ + 16 * g + 16, columns] = spare[
+                    at + g * 160 + a * 16 : at + g * 160 + a * 16 + 16, :
+                ]
+            leaves_ref[a * SQ + 96 : a * SQ + SQ, columns] = spare[at + 960 + 4 * a : at + 964 + 4 * a, :]
+
+    p_row = iota((112, 16), 0)
+    small = iota((112, 16), 1)
     b_of = tenth(p_row)
     c_of = p_row - 10 * b_of
     pick_b = ((b_of == small) & (p_row < SQ)).astype(F32).astype(BF16)
@@ -318,7 +344,7 @@
         [y_filter[0] * z_filter[0], y_filter[1] * z_filter[0], y_filter[0] * z_filter[1], y_filter[1] * z_filter[1]],
         axis=1,
     )
-    ff_high, ff_low = split(ff)
+    ff_both = jnp.concatenate(split(ff), axis=0)
     parent = parent_one_ref[...]
     octant = octant_one_ref[...]
     local = parent - (origin >> 3)
@@ -327,7 +353,8 @@
     code = jnp.where(parent >= 0, code, -1)
     rows = iota((4 * LANES, CAP), 0)
     select = (rows == code).astype(F32).astype(BF16)
-    compress(applied, select, ff_high, ff_low, filter_smem, work, level)
+    compress(leaves_ref, select, ff_both, filter_smem, work, level)
+    leaves_ref[...] = leaves_ref[...] * keep_ref[...].astype(F32)
     parent = parent_two_ref[...]
     octant = octant_two_ref[...]
     local = parent - (origin >> 6)
@@ -340,7 +367,7 @@
     rows = iota((4 * LANES, LANES), 0)
     lane = iota((4 * LANES, LANES), 1)
     select = ((rows == code) & (lane <= 32)).astype(F32).astype(BF16)
-    compress(level, select, ff_high, ff_low, filter_smem, work, level_up)
+    compress(level, select, ff_both, filter_smem, work, level_up)
     one = turned(level, 40)
     two = turned(level_up, 8)
     one_ref[...] = one[:32]
@@ -398,14 +425,13 @@
             pltpu.VMEM((KT, MROWS, LANES), BF16),
             pltpu.VMEM((KT, MROWS, LANES), BF16),
             pltpu.VMEM((2 * KT * LANES, LANES), F32),
+            pltpu.VMEM((10216, LANES), F32),
             pltpu.VMEM((2, KT * LANES, LANES), BF16),
             pltpu.VMEM((2, KT * LANES, LANES), BF16),
             pltpu.VMEM((2 * HALF, LANES), F32),
             pltpu.VMEM((K, 16, 512), F32),
             pltpu.VMEM((K, 16, 512), F32),
             pltpu.VMEM((16, 1024), F32),
-            pltpu.VMEM((MROWS, CAP), F32),
-            pltpu.VMEM((KKK, CAP), F32),
             pltpu.VMEM((KKK, LANES), F32),
             pltpu.VMEM((KKK, LANES), F32),
         ],
@@ -438,15 +464,17 @@
 ):
     terms = operator.reshape(3, 900)
     others = [
-        lax.ppermute(terms, "rank", [(i, (i + step) % 4) for i in range(4)]) for step in (1, 2, 3)
+        lax.ppermute(terms, "rank", [(i, i ^ step) for i in range(4)]) for step in (1, 2, 3)
     ]
-    head, tail = edges(coeffs, neighbours)
+    to_chip, to_next = edges(coeffs, neighbours)
     count = lax.axis_size("box")
-    from_left = lax.ppermute(tail, "box", [(i, i + 1) for i in range(count - 1)])
-    from_right = lax.ppermute(head, "box", [(i + 1, i) for i in range(count - 1)])
+    pairs = [(i, i ^ 1) for i in range(count)]
+    across = [(i, i + 1 if i % 2 else i - 1) for i in range(1, count - 1)]
+    from_chip = lax.ppermute(to_chip, "box", pairs)
+    from_next = lax.ppermute(to_next, "box", across)
     rows = [v[None] for v in (parent_one, octant_one, keep, parent_two, octant_two)]
     leaves, one, two, sent = operator_step(
-        coeffs, from_left, from_right, (terms, *others), (neighbours, *rows), filters
+        coeffs, from_chip, from_next, (terms, *others), (neighbours, *rows), filters
     )
     received = lax.ppermute(sent, "box", [(i + 1, i) for i in range(count - 1)])
     one, two = finish(one, two, received, rows[0], rows[3])

time: 64.3 us -> 61.8 us (0.961); the launches traced: 63.3 us -> 61.6 us
  starting transfers between devices: 17.2 us -> 15.1 us
    ppermute x5, starting transfers between devices: 9.7 us -> 7.43 us  [the longest x1 3.42 us: per_device(): from_next = lax.ppermute(to_next, 'box', across)]
where the time goes in v2:
time: 61.8 us; the launch traced here: 61.6 us
  Pallas kernels  39.6 us (64%)
  starting transfers between devices  15.1 us (24%)
  waiting for transfers between devices  4.64 us (8%)
  local copies, waits for them, and re-layouts  1.51 us (2%)
  between operations  0.74 us (1%)
    pallas_call x1, Pallas kernels, operator_step(): pl.pallas_call(main_kernel, out_shape=(shape((KKK, CAP)), shape((32, KKK)...  35.3 us
    ppermute x1, starting transfers between devices, per_device(): received = lax.ppermute(sent, 'box', [(i + 1, i) for i in range(count - 1)])  7.66 us
    ppermute x3, waiting for transfers between devices, per_device(): lax.ppermute(terms, 'rank', [(i, i ^ step) for i in range(4)])  3.62 us
    ppermute x1, starting transfers between devices, per_device(): from_next = lax.ppermute(to_next, 'box', across)  3.42 us
    ppermute x3, starting transfers between devices, per_device(): lax.ppermute(terms, 'rank', [(i, i ^ step) for i in range(4)])  3.34 us
    pallas_call x1, Pallas kernels, edges(): pl.pallas_call(edges_kernel, out_shape=(shape((HALF, LANES)), shape((HALF...  2.59 us
    pallas_call x1, Pallas kernels, finish(): pl.pallas_call(finish_kernel, out_shape=(shape((32, KKK)), shape((4, KKK)...  1.78 us
    unnamed x17, local copies, waits for them, and re-layouts  1.37 us
  transfers between devices with their start and end apart: 6, of which 3 were waited for; matrix products, arithmetic and copies ran while one was open for 0% of the time, Pallas kernels for 0%

profile of v2, /device:TPU:25, one launch (start us, length us, event | category | flops | bytes accessed | tf_op | source)
XLA Modules:
  0.0 61.6 jit_solution(18073720514892028970)
XLA Ops:
  0.6 0.0 copy-start.2
  0.6 2.6 %edges.1 = (f32[504,128]{1,0:T(8,128)}, f32[504,128]{1,0:T(8,128)}) custom-call(f32[1000,256]{1,0:T(8,128)} %x_ref.3, s32[7,256]{1,0:T(8,128)} %near_ref.1), custom_call_target="tpu_custom_call" | custom-call | tf_op jit(solution)/shard_map/edges/pallas_call | solution.py:408
  3.2 0.7 %collective-permute-start = (f32[504,128]{1,0:T(8,128)}, f32[504,128]{1,0:T(8,128)S(1)}, u32[]{:S(2)}, u32[]{:S(2)}) collective-permute-start(f32[504,128]{1,0:T(8,128)} %get-tuple-element.11), channel_id=1, source_target_pairs={{0,4},{4,0},{8,12},{12,8},{16,20},{20,16},{24,28},{28,24},{32,36},... | collective-permute-start | bytes 774152 | tf_op jit(solution)/shard_map/ppermute | solution.py:473
  3.9 3.4 %collective-permute-start.1 = (f32[504,128]{1,0:T(8,128)}, f32[504,128]{1,0:T(8,128)S(1)}, u32[]{:S(2)}, u32[]{:S(2)}) collective-permute-start(f32[504,128]{1,0:T(8,128)} %get-tuple-element.12), channel_id=1, source_target_pairs={{4,8},{8,4},{12,16},{16,12},{20,24},{24,20},{28,32},{32,28},{36,40... | collective-permute-start | bytes 774152 | tf_op jit(solution)/shard_map/ppermute | solution.py:474
  7.3 0.0 copy-done.2
  7.4 0.1 reshape.9.op0_ref
  7.5 0.0 copy-start.3
  7.5 2.6 %collective-permute-start.4 = (f32[3,900]{1,0:T(4,128)S(1)}, f32[3,900]{1,0:T(4,128)S(1)}, u32[]{:S(2)}, u32[]{:S(2)}) collective-permute-start(f32[3,900]{1,0:T(4,128)S(1)} %reshape.9.op0_ref), channel_id=1, source_target_pairs={{0,3},{1,2},{2,1},{3,0},{4,7},{5,6},{6,5},{7,4},{8,11},{9,10},{10,... | collective-permute-start | bytes 32408 | tf_op jit(solution)/shard_map/ppermute | solution.py:467
  10.1 0.5 collective-permute-start.3
  10.6 0.3 collective-permute-start.2
  10.9 0.5 collective-permute-done.4.op3_ref
  11.4 0.0 copy-start.4
  11.4 3.1 %collective-permute-done.3.op2_ref = f32[3,900]{1,0:T(4,128)S(1)} collective-permute-done((f32[3,900]{1,0:T(4,128)S(1)}, f32[3,900]{1,0:T(4,128)S(1)}, u32[]{:S(2)}, u32[]{:S(2)}) %collective-permute-start.3) | collective-permute-done | bytes 10832 | tf_op jit(solution)/shard_map/ppermute | solution.py:467
  14.5 0.0 copy-start.5
  14.5 0.0 collective-permute-done.2.op1_ref
  14.5 0.0 copy-start.6
  14.5 0.0 collective-permute-done.chip_ref
  14.5 0.0 copy-start
  14.5 0.0 collective-permute-done.1.next_ref
  14.5 0.0 copy-start.1
  14.5 0.0 copy-done.3
  14.5 0.0 copy-done.4
  14.6 0.5 copy-done.5
  15.1 0.0 copy-done.6
  15.1 0.1 copy-done
  15.2 0.1 copy-done.1
  15.3 35.3 %operator.1 = (f32[1000,256]{1,0:T(8,128)}, f32[32,1000]{1,0:T(8,128)}, f32[4,1000]{1,0:T(4,128)}, f32[2,1000]{1,0:T(2,128)}) custom-call(f32[1000,256]{1,0:T(8,128)} %x_ref.3, f32[504,128]{1,0:T(8,128)} %copy-done, f32[504,128]{1,0:T(8,128)} %copy-done.1, f32[3,900]{1,0:T(4,128)} %copy-done.3, f32[3,900]{1,0:T(4,128)} %copy-done.6, f32[3,900]{1,0:T(4,128)} %copy-done.5, ...), custom_call_target="tpu_custom_call" | custom-call | tf_op jit(solution)/shard_map/operator/pallas_call | solution.py:419
  50.6 7.7 %collective-permute-start.5 = (f32[2,1000]{1,0:T(2,128)}, f32[2,1000]{1,0:T(2,128)S(1)}, u32[]{:S(2)}, u32[]{:S(2)}) collective-permute-start(f32[2,1000]{1,0:T(2,128)} %get-tuple-element.16), channel_id=1, source_target_pairs={{4,0},{8,4},{12,8},{16,12},{20,16},{24,20},{28,24},{32,28},{36,32}... | collective-permute-start | bytes 24008 | tf_op jit(solution)/shard_map/ppermute | solution.py:479
  58.2 1.0 %collective-permute-done.5.in_ref = f32[2,1000]{1,0:T(2,128)S(1)} collective-permute-done((f32[2,1000]{1,0:T(2,128)}, f32[2,1000]{1,0:T(2,128)S(1)}, u32[]{:S(2)}, u32[]{:S(2)}) %collective-permute-start.5) | collective-permute-done | bytes 8032 | tf_op jit(solution)/shard_map/ppermute | solution.py:479
  59.2 0.0 copy-start.7
  59.2 0.6 copy-done.7
  59.8 1.8 %finish.1 = (f32[32,1000]{1,0:T(8,128)}, f32[4,1000]{1,0:T(4,128)}) custom-call(f32[32,1000]{1,0:T(8,128)} %get-tuple-element.14.one_ref, f32[4,1000]{1,0:T(4,128)} %get-tuple-element.15.two_ref, f32[2,1000]{1,0:T(2,128)} %copy-done.7, s32[1,256]{1,0:T(1,128)} %bitcast.11, s32[1,32]{1,0:T(1,128)} %bitcast.13), custom_call_target="tpu_custom_call" | custom-call | tf_op jit(solution)/shard_map/finish/pallas_call | solution.py:453
  (1 shorter events, 0.0 us)
Async XLA Ops:
  0.6 6.7 %copy-start.2 = (f32[3,3,3,10,10]{4,2,3,1,0:T(4,128)S(1)}, f32[3,3,3,10,10]{4,2,3,1,0:T(4,128)}, u32[]{:S(2)}) copy-start(f32[3,3,3,10,10]{4,2,3,1,0:T(4,128)} %param.11) | copy-start | bytes 32404
  3.2 11.3 %collective-permute-start = (f32[504,128]{1,0:T(8,128)}, f32[504,128]{1,0:T(8,128)S(1)}, u32[]{:S(2)}, u32[]{:S(2)}) collective-permute-start(f32[504,128]{1,0:T(8,128)} %get-tuple-element.11), channel_id=1, source_target_pairs={{0,4},{4,0},{8,12},{12,8},{16,20},{20,16},{24,28},{28,24},{32,36},... | collective-permute-start | bytes 774152 | tf_op jit(solution)/shard_map/ppermute | solution.py:473
  3.9 10.6 %collective-permute-start.1 = (f32[504,128]{1,0:T(8,128)}, f32[504,128]{1,0:T(8,128)S(1)}, u32[]{:S(2)}, u32[]{:S(2)}) collective-permute-start(f32[504,128]{1,0:T(8,128)} %get-tuple-element.12), channel_id=1, source_target_pairs={{4,8},{8,4},{12,16},{16,12},{20,24},{24,20},{28,32},{32,28},{36,40... | collective-permute-start | bytes 774152 | tf_op jit(solution)/shard_map/ppermute | solution.py:474
  7.5 7.0 %copy-start.3 = (f32[3,900]{1,0:T(4,128)}, f32[3,900]{1,0:T(4,128)S(1)}, u32[]{:S(2)}) copy-start(f32[3,900]{1,0:T(4,128)S(1)} %reshape.9.op0_ref) | copy-start | bytes 32404
  7.5 3.9 %collective-permute-start.4 = (f32[3,900]{1,0:T(4,128)S(1)}, f32[3,900]{1,0:T(4,128)S(1)}, u32[]{:S(2)}, u32[]{:S(2)}) collective-permute-start(f32[3,900]{1,0:T(4,128)S(1)} %reshape.9.op0_ref), channel_id=1, source_target_pairs={{0,3},{1,2},{2,1},{3,0},{4,7},{5,6},{6,5},{7,4},{8,11},{9,10},{10,... | collective-permute-start | bytes 32408 | tf_op jit(solution)/shard_map/ppermute | solution.py:467
  10.1 4.4 %collective-permute-start.3 = (f32[3,900]{1,0:T(4,128)S(1)}, f32[3,900]{1,0:T(4,128)S(1)}, u32[]{:S(2)}, u32[]{:S(2)}) collective-permute-start(f32[3,900]{1,0:T(4,128)S(1)} %reshape.9.op0_ref), channel_id=1, source_target_pairs={{0,2},{1,3},{2,0},{3,1},{4,6},{5,7},{6,4},{7,5},{8,10},{9,11},{10,... | collective-permute-start | bytes 32408 | tf_op jit(solution)/shard_map/ppermute | solution.py:467
  10.6 3.9 %collective-permute-start.2 = (f32[3,900]{1,0:T(4,128)S(1)}, f32[3,900]{1,0:T(4,128)S(1)}, u32[]{:S(2)}, u32[]{:S(2)}) collective-permute-start(f32[3,900]{1,0:T(4,128)S(1)} %reshape.9.op0_ref), channel_id=1, source_target_pairs={{0,1},{1,0},{2,3},{3,2},{4,5},{5,4},{6,7},{7,6},{8,9},{9,8},{10,11... | collective-permute-start | bytes 32408 | tf_op jit(solution)/shard_map/ppermute | solution.py:467
  11.4 3.1 %copy-start.4 = (f32[3,900]{1,0:T(4,128)}, f32[3,900]{1,0:T(4,128)S(1)}, u32[]{:S(2)}) copy-start(f32[3,900]{1,0:T(4,128)S(1)} %collective-permute-done.4.op3_ref) | copy-start | bytes 32404
  14.5 0.6 copy-start.5
  14.5 0.6 copy-start.6
  14.5 0.7 %copy-start = (f32[504,128]{1,0:T(8,128)}, f32[504,128]{1,0:T(8,128)S(1)}, u32[]{:S(2)}) copy-start(f32[504,128]{1,0:T(8,128)S(1)} %collective-permute-done.chip_ref) | copy-start | bytes 774148
  14.5 0.8 %copy-start.1 = (f32[504,128]{1,0:T(8,128)}, f32[504,128]{1,0:T(8,128)S(1)}, u32[]{:S(2)}) copy-start(f32[504,128]{1,0:T(8,128)S(1)} %collective-permute-done.1.next_ref) | copy-start | bytes 774148
  50.6 8.7 %collective-permute-start.5 = (f32[2,1000]{1,0:T(2,128)}, f32[2,1000]{1,0:T(2,128)S(1)}, u32[]{:S(2)}, u32[]{:S(2)}) collective-permute-start(f32[2,1000]{1,0:T(2,128)} %get-tuple-element.16), channel_id=1, source_target_pairs={{4,0},{8,4},{12,8},{16,12},{20,16},{24,20},{28,24},{32,28},{36,32}... | collective-permute-start | bytes 24008 | tf_op jit(solution)/shard_map/ppermute | solution.py:479
  59.2 0.6 copy-start.7

commit v3 on v2

--- a/solution.py
+++ b/solution.py
@@ -20,8 +20,10 @@
 HALF = 504
 LANES = 128
 KT = 60
-MROWS = 1008
-GROUPS = 6
+A_STEP = 101
+TILE = 1016
+I_STEP = 6 * TILE + 1
+DENSE_ROWS = 60984
 
 SAME_X = (0, 3, 4, 5, 6)
 Y_CODE = {0: 0, 3: 1, 4: 2, 5: 0, 6: 0}
@@ -135,10 +137,8 @@
     one_ref,
     two_ref,
     send_ref,
-    w_high,
-    w_low,
+    dense,
     work,
-    spare,
     s_high,
     s_low,
     edge,
@@ -224,96 +224,65 @@
             s_high[h, 512 * t : 512 * (t + 1), :] = high
             s_low[h, 512 * t : 512 * (t + 1), :] = low
 
-    def build(stage, pair_of, count, step, width, between):
-        apart = 6 * width + 1
-
-        def put(value, first_tile, position, tiles):
-            for l in range(tiles):
-                at = (first_tile + l) * width + position
-                part = value[:, l * LANES : (l + 1) * LANES]
-                for a in range(K):
-                    stage[pl.ds(at + a * step, 8, stride=apart), :] = part[8 * a : 8 * a + 8]
-                for n, i in enumerate((8, 9)):
-                    stage[pl.ds(at + i * apart, 8, stride=step), :] = part[80 + 8 * n : 88 + 8 * n]
-                for n, a in enumerate((8, 9)):
-                    stage[pl.ds(at + 8 * apart + a * step, 2, stride=apart), :] = part[
-                        96 + 2 * n : 98 + 2 * n
-                    ]
-
+    def put(value, l, p):
+        at = l * TILE + p
+        for a in range(K):
+            dense[pl.ds(at + a * A_STEP, 8, stride=I_STEP), :] = value[8 * a : 8 * a + 8]
+        for n, i in enumerate((8, 9)):
+            dense[pl.ds(at + i * I_STEP, 8, stride=A_STEP), :] = value[80 + 8 * n : 88 + 8 * n]
+        for n, a in enumerate((8, 9)):
+            dense[pl.ds(at + 8 * I_STEP + a * A_STEP, 2, stride=I_STEP), :] = value[
+                96 + 2 * n : 98 + 2 * n
+            ]
+
+    def one_b(b, carry):
+        y_part = b_wide[b]
         held = []
-        for u in range(count):
-            b, c = pair_of(u)
-            high, low = split(b_wide[b] * c_wide[c])
+        for c in range(K):
+            p = b * K + c
+            high, low = split(y_part * c_wide[c])
             rhs = jnp.concatenate([high, high, low], axis=0)
             for part in range(2):
-                put(mm(x_same, rhs[:, 256 * part : 256 * part + 256]), 2 * part, u, 2)
+                both = mm(x_same, rhs[:, 256 * part : 256 * part + 256])
+                for n in range(2):
+                    put(both[:, n * LANES : (n + 1) * LANES], 2 * part + n, p)
             held.append(rhs[:, :LANES])
             if len(held) == 2:
                 both = mm(x_moved, jnp.concatenate(held, axis=1))
                 for n in range(2):
-                    put(both[:104, n * LANES : (n + 1) * LANES], 4, u - 1 + n, 1)
-                    put(both[104:, n * LANES : (n + 1) * LANES], 5, u - 1 + n, 1)
+                    put(both[:104, n * LANES : (n + 1) * LANES], 4, p - 1 + n)
+                    put(both[104:, n * LANES : (n + 1) * LANES], 5, p - 1 + n)
                 held = []
-            between(u)
-
-    def pair_in(g):
-        def pair_of(u):
-            p = g * 16 + u
-            b = (p * 205) >> 11
-            return b, p - 10 * b
-
-        return pair_of
-
-    def convert(stage, g, count):
-        first = pl.multiple_of(g * 160, 160)
-
-        def between(u):
-            for unit in range(u * KT * K // count, (u + 1) * KT * K // count):
-                t, a = divmod(unit, K)
-                at = (t // 6) * 1021 + (t % 6) * 170 + 17 * a
-                high, low = split(stage[at : at + 16, :])
-                w_high[t, pl.ds(first + 16 * a, 16), :] = high
-                w_low[t, pl.ds(first + 16 * a, 16), :] = low
-
-        return between
-
-    def two_groups(n, carry):
-        g = 2 * n
-        ahead = jnp.where(n == 0, GROUPS - 1, g - 1)
-        build(work, pair_in(g), 16, 17, 170, convert(spare, ahead, 16))
-        build(spare, pair_in(g + 1), 16, 17, 170, convert(work, g, 16))
         return carry
 
-    lax.fori_loop(0, GROUPS // 2, two_groups, 0)
-    build(work, lambda u: (9, 6 + u), 4, 4, 48, convert(spare, GROUPS - 1, 4))
-    for t in range(KT):
-        at = (t // 6) * 289 + (t % 6) * 48
-        high, low = split(work[at : at + 48, :])
-        w_high[t, 960:MROWS, :] = high
-        w_low[t, 960:MROWS, :] = low
-
-    tall_high = jnp.concatenate([s_high[0], s_high[1]], axis=1)
-    tall_low = jnp.concatenate([s_low[0], s_low[1]], axis=1)
-    middle = KT // 2
-    first = [w_high[t] for t in range(KT)] + [w_low[t] for t in range(middle)]
-    second = [w_low[t] for t in range(middle, KT)] + [w_high[t] for t in range(KT)]
-    total = mm(
-        jnp.concatenate(first, axis=1),
-        jnp.concatenate([tall_high, tall_high[: middle * LANES]], axis=0),
-    ) + mm(
-        jnp.concatenate(second, axis=1),
-        jnp.concatenate([tall_high[middle * LANES :], tall_low], axis=0),
-    )
+    lax.fori_loop(0, K, one_b, 0)
+
+    for pair in range(5):
+        at = 2 * pair * 768
+        tall_high = jnp.concatenate([s_high[h, at : at + 1536, :] for h in range(2)], axis=1)
+        tall_low = jnp.concatenate([s_low[h, at : at + 1536, :] for h in range(2)], axis=1)
+        tall = jnp.concatenate([tall_high, tall_high, tall_low], axis=0)
+        for m in range(2):
+            highs = []
+            lows = []
+            for i in (2 * pair, 2 * pair + 1):
+                for l in range(6):
+                    first = i * I_STEP + l * TILE + 512 * m
+                    high, low = split(dense[first : first + 512, :])
+                    highs.append(high)
+                    lows.append(low)
+            total = mm(jnp.concatenate(highs + lows + highs, axis=1), tall)
+            for h in range(2):
+                rows = slice(h * 1024 + 512 * m, h * 1024 + 512 * m + 512)
+                part = total[:, h * LANES : (h + 1) * LANES]
+                if pair == 0:
+                    work[rows, :] = part
+                else:
+                    work[rows, :] += part
     for h in range(2):
-        at = h * MROWS
-        columns = slice(h * LANES, (h + 1) * LANES)
-        spare[at : at + MROWS, :] = total[:, columns]
         for a in range(K):
-            for g in range(GROUPS):
-                leaves_ref[a * SQ + 16 * g : a * SQ + 16 * g + 16, columns] = spare[
-                    at + g * 160 + a * 16 : at + g * 160 + a * 16 + 16, :
-                ]
-            leaves_ref[a * SQ + 96 : a * SQ + SQ, columns] = spare[at + 960 + 4 * a : at + 964 + 4 * a, :]
+            first = h * 1024 + a * A_STEP
+            leaves_ref[a * SQ : (a + 1) * SQ, h * LANES : (h + 1) * LANES] = work[first : first + SQ, :]
 
     p_row = iota((112, 16), 0)
     small = iota((112, 16), 1)
@@ -422,10 +391,8 @@
         in_specs=[VMEM_SPEC] * 15 + [SMEM_SPEC],
         out_specs=(VMEM_SPEC,) * 4,
         scratch_shapes=[
-            pltpu.VMEM((KT, MROWS, LANES), BF16),
-            pltpu.VMEM((KT, MROWS, LANES), BF16),
+            pltpu.VMEM((DENSE_ROWS, LANES), F32),
             pltpu.VMEM((2 * KT * LANES, LANES), F32),
-            pltpu.VMEM((10216, LANES), F32),
             pltpu.VMEM((2, KT * LANES, LANES), BF16),
             pltpu.VMEM((2, KT * LANES, LANES), BF16),
             pltpu.VMEM((2 * HALF, LANES), F32),

time: 61.8 us -> 54.8 us (0.89)
  Pallas kernels: 39.6 us -> 32.6 us
    pallas_call x1, Pallas kernels: 35.3 us -> 28.2 us  [operator_step(): pl.pallas_call(main_kernel, out_shape=(shape((KKK, CAP)), shape((32, KKK)...]
where the time goes in v3:
time: 54.8 us; the launch traced here: 54.6 us
  Pallas kernels  32.6 us (59%)
  starting transfers between devices  15.1 us (28%)
  waiting for transfers between devices  4.64 us (8%)
  local copies, waits for them, and re-layouts  1.51 us (3%)
  between operations  0.74 us (1%)
    pallas_call x1, Pallas kernels, operator_step(): pl.pallas_call(main_kernel, out_shape=(shape((KKK, CAP)), shape((32, KKK)...  28.2 us
    ppermute x1, starting transfers between devices, per_device(): received = lax.ppermute(sent, 'box', [(i + 1, i) for i in range(count - 1)])  7.66 us
    ppermute x3, waiting for transfers between devices, per_device(): lax.ppermute(terms, 'rank', [(i, i ^ step) for i in range(4)])  3.62 us
    ppermute x1, starting transfers between devices, per_device(): from_next = lax.ppermute(to_next, 'box', across)  3.42 us
    ppermute x3, starting transfers between devices, per_device(): lax.ppermute(terms, 'rank', [(i, i ^ step) for i in range(4)])  3.34 us
    pallas_call x1, Pallas kernels, edges(): pl.pallas_call(edges_kernel, out_shape=(shape((HALF, LANES)), shape((HALF...  2.59 us
    pallas_call x1, Pallas kernels, finish(): pl.pallas_call(finish_kernel, out_shape=(shape((32, KKK)), shape((4, KKK)...  1.78 us
    unnamed x17, local copies, waits for them, and re-layouts  1.37 us
  transfers between devices with their start and end apart: 6, of which 3 were waited for; matrix products, arithmetic and copies ran while one was open for 0% of the time, Pallas kernels for 0%

profile of v3, /device:TPU:25, one launch (start us, length us, event | category | flops | bytes accessed | tf_op | source)
XLA Modules:
  0.0 54.6 jit_solution(1677023862719657140)
XLA Ops:
  0.6 0.0 copy-start.2
  0.6 2.6 %edges.1 = (f32[504,128]{1,0:T(8,128)}, f32[504,128]{1,0:T(8,128)}) custom-call(f32[1000,256]{1,0:T(8,128)} %x_ref.3, s32[7,256]{1,0:T(8,128)} %near_ref.1), custom_call_target="tpu_custom_call" | custom-call | tf_op jit(solution)/shard_map/edges/pallas_call | solution.py:377
  3.2 0.7 %collective-permute-start = (f32[504,128]{1,0:T(8,128)}, f32[504,128]{1,0:T(8,128)S(1)}, u32[]{:S(2)}, u32[]{:S(2)}) collective-permute-start(f32[504,128]{1,0:T(8,128)} %get-tuple-element.11), channel_id=1, source_target_pairs={{0,4},{4,0},{8,12},{12,8},{16,20},{20,16},{24,28},{28,24},{32,36},... | collective-permute-start | bytes 774152 | tf_op jit(solution)/shard_map/ppermute | solution.py:440
  3.9 3.4 %collective-permute-start.1 = (f32[504,128]{1,0:T(8,128)}, f32[504,128]{1,0:T(8,128)S(1)}, u32[]{:S(2)}, u32[]{:S(2)}) collective-permute-start(f32[504,128]{1,0:T(8,128)} %get-tuple-element.12), channel_id=1, source_target_pairs={{4,8},{8,4},{12,16},{16,12},{20,24},{24,20},{28,32},{32,28},{36,40... | collective-permute-start | bytes 774152 | tf_op jit(solution)/shard_map/ppermute | solution.py:441
  7.3 0.0 copy-done.2
  7.4 0.1 reshape.9.op0_ref
  7.5 0.0 copy-start.3
  7.5 2.6 %collective-permute-start.4 = (f32[3,900]{1,0:T(4,128)S(1)}, f32[3,900]{1,0:T(4,128)S(1)}, u32[]{:S(2)}, u32[]{:S(2)}) collective-permute-start(f32[3,900]{1,0:T(4,128)S(1)} %reshape.9.op0_ref), channel_id=1, source_target_pairs={{0,3},{1,2},{2,1},{3,0},{4,7},{5,6},{6,5},{7,4},{8,11},{9,10},{10,... | collective-permute-start | bytes 32408 | tf_op jit(solution)/shard_map/ppermute | solution.py:434
  10.1 0.5 collective-permute-start.3
  10.6 0.3 collective-permute-start.2
  10.9 0.5 collective-permute-done.4.op3_ref
  11.4 0.0 copy-start.4
  11.4 3.1 %collective-permute-done.3.op2_ref = f32[3,900]{1,0:T(4,128)S(1)} collective-permute-done((f32[3,900]{1,0:T(4,128)S(1)}, f32[3,900]{1,0:T(4,128)S(1)}, u32[]{:S(2)}, u32[]{:S(2)}) %collective-permute-start.3) | collective-permute-done | bytes 10832 | tf_op jit(solution)/shard_map/ppermute | solution.py:434
  14.5 0.0 copy-start.5
  14.5 0.0 collective-permute-done.2.op1_ref
  14.5 0.0 copy-start.6
  14.5 0.0 collective-permute-done.chip_ref
  14.5 0.0 copy-start
  14.5 0.0 collective-permute-done.1.next_ref
  14.5 0.0 copy-start.1
  14.5 0.0 copy-done.3
  14.5 0.0 copy-done.4
  14.6 0.5 copy-done.5
  15.1 0.0 copy-done.6
  15.1 0.1 copy-done
  15.2 0.1 copy-done.1
  15.3 28.2 %operator.1 = (f32[1000,256]{1,0:T(8,128)}, f32[32,1000]{1,0:T(8,128)}, f32[4,1000]{1,0:T(4,128)}, f32[2,1000]{1,0:T(2,128)}) custom-call(f32[1000,256]{1,0:T(8,128)} %x_ref.3, f32[504,128]{1,0:T(8,128)} %copy-done, f32[504,128]{1,0:T(8,128)} %copy-done.1, f32[3,900]{1,0:T(4,128)} %copy-done.3, f32[3,900]{1,0:T(4,128)} %copy-done.6, f32[3,900]{1,0:T(4,128)} %copy-done.5, ...), custom_call_target="tpu_custom_call" | custom-call | tf_op jit(solution)/shard_map/operator/pallas_call | solution.py:388
  43.5 7.7 %collective-permute-start.5 = (f32[2,1000]{1,0:T(2,128)}, f32[2,1000]{1,0:T(2,128)S(1)}, u32[]{:S(2)}, u32[]{:S(2)}) collective-permute-start(f32[2,1000]{1,0:T(2,128)} %get-tuple-element.16), channel_id=1, source_target_pairs={{4,0},{8,4},{12,8},{16,12},{20,16},{24,20},{28,24},{32,28},{36,32}... | collective-permute-start | bytes 24008 | tf_op jit(solution)/shard_map/ppermute | solution.py:446
  51.2 1.0 %collective-permute-done.5.in_ref = f32[2,1000]{1,0:T(2,128)S(1)} collective-permute-done((f32[2,1000]{1,0:T(2,128)}, f32[2,1000]{1,0:T(2,128)S(1)}, u32[]{:S(2)}, u32[]{:S(2)}) %collective-permute-start.5) | collective-permute-done | bytes 8032 | tf_op jit(solution)/shard_map/ppermute | solution.py:446
  52.2 0.0 copy-start.7
  52.2 0.6 %copy-done.7 = f32[2,1000]{1,0:T(2,128)} copy-done((f32[2,1000]{1,0:T(2,128)}, f32[2,1000]{1,0:T(2,128)S(1)}, u32[]{:S(2)}) %copy-start.7) | copy-done | bytes 8024
  52.8 1.8 %finish.1 = (f32[32,1000]{1,0:T(8,128)}, f32[4,1000]{1,0:T(4,128)}) custom-call(f32[32,1000]{1,0:T(8,128)} %get-tuple-element.14.one_ref, f32[4,1000]{1,0:T(4,128)} %get-tuple-element.15.two_ref, f32[2,1000]{1,0:T(2,128)} %copy-done.7, s32[1,256]{1,0:T(1,128)} %bitcast.11, s32[1,32]{1,0:T(1,128)} %bitcast.13), custom_call_target="tpu_custom_call" | custom-call | tf_op jit(solution)/shard_map/finish/pallas_call | solution.py:420
  (1 shorter events, 0.0 us)
Async XLA Ops:
  0.6 6.7 %copy-start.2 = (f32[3,3,3,10,10]{4,2,3,1,0:T(4,128)S(1)}, f32[3,3,3,10,10]{4,2,3,1,0:T(4,128)}, u32[]{:S(2)}) copy-start(f32[3,3,3,10,10]{4,2,3,1,0:T(4,128)} %param.11) | copy-start | bytes 32404
  3.2 11.3 %collective-permute-start = (f32[504,128]{1,0:T(8,128)}, f32[504,128]{1,0:T(8,128)S(1)}, u32[]{:S(2)}, u32[]{:S(2)}) collective-permute-start(f32[504,128]{1,0:T(8,128)} %get-tuple-element.11), channel_id=1, source_target_pairs={{0,4},{4,0},{8,12},{12,8},{16,20},{20,16},{24,28},{28,24},{32,36},... | collective-permute-start | bytes 774152 | tf_op jit(solution)/shard_map/ppermute | solution.py:440
  3.9 10.6 %collective-permute-start.1 = (f32[504,128]{1,0:T(8,128)}, f32[504,128]{1,0:T(8,128)S(1)}, u32[]{:S(2)}, u32[]{:S(2)}) collective-permute-start(f32[504,128]{1,0:T(8,128)} %get-tuple-element.12), channel_id=1, source_target_pairs={{4,8},{8,4},{12,16},{16,12},{20,24},{24,20},{28,32},{32,28},{36,40... | collective-permute-start | bytes 774152 | tf_op jit(solution)/shard_map/ppermute | solution.py:441
  7.5 7.0 %copy-start.3 = (f32[3,900]{1,0:T(4,128)}, f32[3,900]{1,0:T(4,128)S(1)}, u32[]{:S(2)}) copy-start(f32[3,900]{1,0:T(4,128)S(1)} %reshape.9.op0_ref) | copy-start | bytes 32404
  7.5 3.9 %collective-permute-start.4 = (f32[3,900]{1,0:T(4,128)S(1)}, f32[3,900]{1,0:T(4,128)S(1)}, u32[]{:S(2)}, u32[]{:S(2)}) collective-permute-start(f32[3,900]{1,0:T(4,128)S(1)} %reshape.9.op0_ref), channel_id=1, source_target_pairs={{0,3},{1,2},{2,1},{3,0},{4,7},{5,6},{6,5},{7,4},{8,11},{9,10},{10,... | collective-permute-start | bytes 32408 | tf_op jit(solution)/shard_map/ppermute | solution.py:434
  10.1 4.4 %collective-permute-start.3 = (f32[3,900]{1,0:T(4,128)S(1)}, f32[3,900]{1,0:T(4,128)S(1)}, u32[]{:S(2)}, u32[]{:S(2)}) collective-permute-start(f32[3,900]{1,0:T(4,128)S(1)} %reshape.9.op0_ref), channel_id=1, source_target_pairs={{0,2},{1,3},{2,0},{3,1},{4,6},{5,7},{6,4},{7,5},{8,10},{9,11},{10,... | collective-permute-start | bytes 32408 | tf_op jit(solution)/shard_map/ppermute | solution.py:434
  10.6 3.9 %collective-permute-start.2 = (f32[3,900]{1,0:T(4,128)S(1)}, f32[3,900]{1,0:T(4,128)S(1)}, u32[]{:S(2)}, u32[]{:S(2)}) collective-permute-start(f32[3,900]{1,0:T(4,128)S(1)} %reshape.9.op0_ref), channel_id=1, source_target_pairs={{0,1},{1,0},{2,3},{3,2},{4,5},{5,4},{6,7},{7,6},{8,9},{9,8},{10,11... | collective-permute-start | bytes 32408 | tf_op jit(solution)/shard_map/ppermute | solution.py:434
  11.4 3.1 %copy-start.4 = (f32[3,900]{1,0:T(4,128)}, f32[3,900]{1,0:T(4,128)S(1)}, u32[]{:S(2)}) copy-start(f32[3,900]{1,0:T(4,128)S(1)} %collective-permute-done.4.op3_ref) | copy-start | bytes 32404
  14.5 0.6 %copy-start.5 = (f32[3,900]{1,0:T(4,128)}, f32[3,900]{1,0:T(4,128)S(1)}, u32[]{:S(2)}) copy-start(f32[3,900]{1,0:T(4,128)S(1)} %collective-permute-done.3.op2_ref) | copy-start | bytes 32404
  14.5 0.6 %copy-start.6 = (f32[3,900]{1,0:T(4,128)}, f32[3,900]{1,0:T(4,128)S(1)}, u32[]{:S(2)}) copy-start(f32[3,900]{1,0:T(4,128)S(1)} %collective-permute-done.2.op1_ref) | copy-start | bytes 32404
  14.5 0.7 %copy-start = (f32[504,128]{1,0:T(8,128)}, f32[504,128]{1,0:T(8,128)S(1)}, u32[]{:S(2)}) copy-start(f32[504,128]{1,0:T(8,128)S(1)} %collective-permute-done.chip_ref) | copy-start | bytes 774148
  14.5 0.8 %copy-start.1 = (f32[504,128]{1,0:T(8,128)}, f32[504,128]{1,0:T(8,128)S(1)}, u32[]{:S(2)}) copy-start(f32[504,128]{1,0:T(8,128)S(1)} %collective-permute-done.1.next_ref) | copy-start | bytes 774148
  43.5 8.7 %collective-permute-start.5 = (f32[2,1000]{1,0:T(2,128)}, f32[2,1000]{1,0:T(2,128)S(1)}, u32[]{:S(2)}, u32[]{:S(2)}) collective-permute-start(f32[2,1000]{1,0:T(2,128)} %get-tuple-element.16), channel_id=1, source_target_pairs={{4,0},{8,4},{12,8},{16,12},{20,16},{24,20},{28,24},{32,28},{36,32}... | collective-permute-start | bytes 24008 | tf_op jit(solution)/shard_map/ppermute | solution.py:446
  52.2 0.6 %copy-start.7 = (f32[2,1000]{1,0:T(2,128)}, f32[2,1000]{1,0:T(2,128)S(1)}, u32[]{:S(2)}) copy-start(f32[2,1000]{1,0:T(2,128)S(1)} %collective-permute-done.5.in_ref) | copy-start | bytes 24004

commit v4 on v3

--- a/solution.py
+++ b/solution.py
@@ -50,6 +50,10 @@
 
 def iota(shape, dim):
     return lax.broadcasted_iota(I32, shape, dim)
+
+
+def place_of(a):
+    return a * A_STEP - max(a - 7, 0)
 
 
 def tenth(index):
@@ -227,11 +231,11 @@
     def put(value, l, p):
         at = l * TILE + p
         for a in range(K):
-            dense[pl.ds(at + a * A_STEP, 8, stride=I_STEP), :] = value[8 * a : 8 * a + 8]
+            dense[pl.ds(at + place_of(a), 8, stride=I_STEP), :] = value[8 * a : 8 * a + 8]
         for n, i in enumerate((8, 9)):
             dense[pl.ds(at + i * I_STEP, 8, stride=A_STEP), :] = value[80 + 8 * n : 88 + 8 * n]
         for n, a in enumerate((8, 9)):
-            dense[pl.ds(at + 8 * I_STEP + a * A_STEP, 2, stride=I_STEP), :] = value[
+            dense[pl.ds(at + 8 * I_STEP + place_of(a), 2, stride=I_STEP), :] = value[
                 96 + 2 * n : 98 + 2 * n
             ]
 
@@ -268,12 +272,12 @@
             for i in (2 * pair, 2 * pair + 1):
                 for l in range(6):
                     first = i * I_STEP + l * TILE + 512 * m
-                    high, low = split(dense[first : first + 512, :])
+                    high, low = split(dense[first : first + 512 - 16 * m, :])
                     highs.append(high)
                     lows.append(low)
             total = mm(jnp.concatenate(highs + lows + highs, axis=1), tall)
             for h in range(2):
-                rows = slice(h * 1024 + 512 * m, h * 1024 + 512 * m + 512)
+                rows = slice(h * 1024 + 512 * m, h * 1024 + 1024 * m + 512 * (1 - m) - 16 * m)
                 part = total[:, h * LANES : (h + 1) * LANES]
                 if pair == 0:
                     work[rows, :] = part
@@ -281,7 +285,7 @@
                     work[rows, :] += part
     for h in range(2):
         for a in range(K):
-            first = h * 1024 + a * A_STEP
+            first = h * 1024 + place_of(a)
             leaves_ref[a * SQ : (a + 1) * SQ, h * LANES : (h + 1) * LANES] = work[first : first + SQ, :]
 
     p_row = iota((112, 16), 0)

time: 54.8 us -> 54.2 us (0.989)
  Pallas kernels: 32.6 us -> 32 us
    pallas_call x1, Pallas kernels: 28.2 us -> 27.6 us  [operator_step(): pl.pallas_call(main_kernel, out_shape=(shape((KKK, CAP)), shape((32, KKK)...]
where the time goes in v4:
time: 54.2 us; the launch traced here: 54 us
  Pallas kernels  32 us (59%)
  starting transfers between devices  15.1 us (28%)
  waiting for transfers between devices  4.64 us (9%)
  local copies, waits for them, and re-layouts  1.51 us (3%)
  between operations  0.74 us (1%)
    pallas_call x1, Pallas kernels, operator_step(): pl.pallas_call(main_kernel, out_shape=(shape((KKK, CAP)), shape((32, KKK)...  27.6 us
    ppermute x1, starting transfers between devices, per_device(): received = lax.ppermute(sent, 'box', [(i + 1, i) for i in range(count - 1)])  7.66 us
    ppermute x3, waiting for transfers between devices, per_device(): lax.ppermute(terms, 'rank', [(i, i ^ step) for i in range(4)])  3.62 us
    ppermute x1, starting transfers between devices, per_device(): from_next = lax.ppermute(to_next, 'box', across)  3.42 us
    ppermute x3, starting transfers between devices, per_device(): lax.ppermute(terms, 'rank', [(i, i ^ step) for i in range(4)])  3.34 us
    pallas_call x1, Pallas kernels, edges(): pl.pallas_call(edges_kernel, out_shape=(shape((HALF, LANES)), shape((HALF...  2.59 us
    pallas_call x1, Pallas kernels, finish(): pl.pallas_call(finish_kernel, out_shape=(shape((32, KKK)), shape((4, KKK)...  1.78 us
    unnamed x17, local copies, waits for them, and re-layouts  1.37 us
  transfers between devices with their start and end apart: 6, of which 3 were waited for; matrix products, arithmetic and copies ran while one was open for 0% of the time, Pallas kernels for 0%

profile of v4, /device:TPU:25, one launch (start us, length us, event | category | flops | bytes accessed | tf_op | source)
XLA Modules:
  0.0 54.0 jit_solution(5852557504814748197)
XLA Ops:
  0.6 0.0 copy-start.2
  0.6 2.6 %edges.1 = (f32[504,128]{1,0:T(8,128)}, f32[504,128]{1,0:T(8,128)}) custom-call(f32[1000,256]{1,0:T(8,128)} %x_ref.3, s32[7,256]{1,0:T(8,128)} %near_ref.1), custom_call_target="tpu_custom_call" | custom-call | tf_op jit(solution)/shard_map/edges/pallas_call | solution.py:381
  3.2 0.7 %collective-permute-start = (f32[504,128]{1,0:T(8,128)}, f32[504,128]{1,0:T(8,128)S(1)}, u32[]{:S(2)}, u32[]{:S(2)}) collective-permute-start(f32[504,128]{1,0:T(8,128)} %get-tuple-element.11), channel_id=1, source_target_pairs={{0,4},{4,0},{8,12},{12,8},{16,20},{20,16},{24,28},{28,24},{32,36},... | collective-permute-start | bytes 774152 | tf_op jit(solution)/shard_map/ppermute | solution.py:444
  3.9 3.4 %collective-permute-start.1 = (f32[504,128]{1,0:T(8,128)}, f32[504,128]{1,0:T(8,128)S(1)}, u32[]{:S(2)}, u32[]{:S(2)}) collective-permute-start(f32[504,128]{1,0:T(8,128)} %get-tuple-element.12), channel_id=1, source_target_pairs={{4,8},{8,4},{12,16},{16,12},{20,24},{24,20},{28,32},{32,28},{36,40... | collective-permute-start | bytes 774152 | tf_op jit(solution)/shard_map/ppermute | solution.py:445
  7.3 0.0 copy-done.2
  7.4 0.1 reshape.9.op0_ref
  7.5 0.0 copy-start.3
  7.5 2.6 %collective-permute-start.4 = (f32[3,900]{1,0:T(4,128)S(1)}, f32[3,900]{1,0:T(4,128)S(1)}, u32[]{:S(2)}, u32[]{:S(2)}) collective-permute-start(f32[3,900]{1,0:T(4,128)S(1)} %reshape.9.op0_ref), channel_id=1, source_target_pairs={{0,3},{1,2},{2,1},{3,0},{4,7},{5,6},{6,5},{7,4},{8,11},{9,10},{10,... | collective-permute-start | bytes 32408 | tf_op jit(solution)/shard_map/ppermute | solution.py:438
  10.1 0.5 collective-permute-start.3
  10.6 0.3 collective-permute-start.2
  10.9 0.5 %collective-permute-done.4.op3_ref = f32[3,900]{1,0:T(4,128)S(1)} collective-permute-done((f32[3,900]{1,0:T(4,128)S(1)}, f32[3,900]{1,0:T(4,128)S(1)}, u32[]{:S(2)}, u32[]{:S(2)}) %collective-permute-start.4) | collective-permute-done | bytes 10832 | tf_op jit(solution)/shard_map/ppermute | solution.py:438
  11.4 0.0 copy-start.4
  11.4 3.1 %collective-permute-done.3.op2_ref = f32[3,900]{1,0:T(4,128)S(1)} collective-permute-done((f32[3,900]{1,0:T(4,128)S(1)}, f32[3,900]{1,0:T(4,128)S(1)}, u32[]{:S(2)}, u32[]{:S(2)}) %collective-permute-start.3) | collective-permute-done | bytes 10832 | tf_op jit(solution)/shard_map/ppermute | solution.py:438
  14.5 0.0 copy-start.5
  14.5 0.0 collective-permute-done.2.op1_ref
  14.5 0.0 copy-start.6
  14.5 0.0 collective-permute-done.chip_ref
  14.5 0.0 copy-start
  14.5 0.0 collective-permute-done.1.next_ref
  14.5 0.0 copy-start.1
  14.5 0.0 copy-done.3
  14.5 0.0 copy-done.4
  14.6 0.5 copy-done.5
  15.1 0.0 copy-done.6
  15.1 0.1 copy-done
  15.2 0.1 copy-done.1
  15.3 27.6 %operator.1 = (f32[1000,256]{1,0:T(8,128)}, f32[32,1000]{1,0:T(8,128)}, f32[4,1000]{1,0:T(4,128)}, f32[2,1000]{1,0:T(2,128)}) custom-call(f32[1000,256]{1,0:T(8,128)} %x_ref.3, f32[504,128]{1,0:T(8,128)} %copy-done, f32[504,128]{1,0:T(8,128)} %copy-done.1, f32[3,900]{1,0:T(4,128)} %copy-done.3, f32[3,900]{1,0:T(4,128)} %copy-done.6, f32[3,900]{1,0:T(4,128)} %copy-done.5, ...), custom_call_target="tpu_custom_call" | custom-call | tf_op jit(solution)/shard_map/operator/pallas_call | solution.py:392
  42.9 7.7 %collective-permute-start.5 = (f32[2,1000]{1,0:T(2,128)}, f32[2,1000]{1,0:T(2,128)S(1)}, u32[]{:S(2)}, u32[]{:S(2)}) collective-permute-start(f32[2,1000]{1,0:T(2,128)} %get-tuple-element.16), channel_id=1, source_target_pairs={{4,0},{8,4},{12,8},{16,12},{20,16},{24,20},{28,24},{32,28},{36,32}... | collective-permute-start | bytes 24008 | tf_op jit(solution)/shard_map/ppermute | solution.py:450
  50.6 1.0 %collective-permute-done.5.in_ref = f32[2,1000]{1,0:T(2,128)S(1)} collective-permute-done((f32[2,1000]{1,0:T(2,128)}, f32[2,1000]{1,0:T(2,128)S(1)}, u32[]{:S(2)}, u32[]{:S(2)}) %collective-permute-start.5) | collective-permute-done | bytes 8032 | tf_op jit(solution)/shard_map/ppermute | solution.py:450
  51.6 0.0 copy-start.7
  51.6 0.6 %copy-done.7 = f32[2,1000]{1,0:T(2,128)} copy-done((f32[2,1000]{1,0:T(2,128)}, f32[2,1000]{1,0:T(2,128)S(1)}, u32[]{:S(2)}) %copy-start.7) | copy-done | bytes 8024
  52.2 1.8 %finish.1 = (f32[32,1000]{1,0:T(8,128)}, f32[4,1000]{1,0:T(4,128)}) custom-call(f32[32,1000]{1,0:T(8,128)} %get-tuple-element.14.one_ref, f32[4,1000]{1,0:T(4,128)} %get-tuple-element.15.two_ref, f32[2,1000]{1,0:T(2,128)} %copy-done.7, s32[1,256]{1,0:T(1,128)} %bitcast.11, s32[1,32]{1,0:T(1,128)} %bitcast.13), custom_call_target="tpu_custom_call" | custom-call | tf_op jit(solution)/shard_map/finish/pallas_call | solution.py:424
  (1 shorter events, 0.0 us)
Async XLA Ops:
  0.6 6.7 %copy-start.2 = (f32[3,3,3,10,10]{4,2,3,1,0:T(4,128)S(1)}, f32[3,3,3,10,10]{4,2,3,1,0:T(4,128)}, u32[]{:S(2)}) copy-start(f32[3,3,3,10,10]{4,2,3,1,0:T(4,128)} %param.11) | copy-start | bytes 32404
  3.2 11.3 %collective-permute-start = (f32[504,128]{1,0:T(8,128)}, f32[504,128]{1,0:T(8,128)S(1)}, u32[]{:S(2)}, u32[]{:S(2)}) collective-permute-start(f32[504,128]{1,0:T(8,128)} %get-tuple-element.11), channel_id=1, source_target_pairs={{0,4},{4,0},{8,12},{12,8},{16,20},{20,16},{24,28},{28,24},{32,36},... | collective-permute-start | bytes 774152 | tf_op jit(solution)/shard_map/ppermute | solution.py:444
  3.9 10.6 %collective-permute-start.1 = (f32[504,128]{1,0:T(8,128)}, f32[504,128]{1,0:T(8,128)S(1)}, u32[]{:S(2)}, u32[]{:S(2)}) collective-permute-start(f32[504,128]{1,0:T(8,128)} %get-tuple-element.12), channel_id=1, source_target_pairs={{4,8},{8,4},{12,16},{16,12},{20,24},{24,20},{28,32},{32,28},{36,40... | collective-permute-start | bytes 774152 | tf_op jit(solution)/shard_map/ppermute | solution.py:445
  7.5 7.0 %copy-start.3 = (f32[3,900]{1,0:T(4,128)}, f32[3,900]{1,0:T(4,128)S(1)}, u32[]{:S(2)}) copy-start(f32[3,900]{1,0:T(4,128)S(1)} %reshape.9.op0_ref) | copy-start | bytes 32404
  7.5 3.9 %collective-permute-start.4 = (f32[3,900]{1,0:T(4,128)S(1)}, f32[3,900]{1,0:T(4,128)S(1)}, u32[]{:S(2)}, u32[]{:S(2)}) collective-permute-start(f32[3,900]{1,0:T(4,128)S(1)} %reshape.9.op0_ref), channel_id=1, source_target_pairs={{0,3},{1,2},{2,1},{3,0},{4,7},{5,6},{6,5},{7,4},{8,11},{9,10},{10,... | collective-permute-start | bytes 32408 | tf_op jit(solution)/shard_map/ppermute | solution.py:438
  10.1 4.4 %collective-permute-start.3 = (f32[3,900]{1,0:T(4,128)S(1)}, f32[3,900]{1,0:T(4,128)S(1)}, u32[]{:S(2)}, u32[]{:S(2)}) collective-permute-start(f32[3,900]{1,0:T(4,128)S(1)} %reshape.9.op0_ref), channel_id=1, source_target_pairs={{0,2},{1,3},{2,0},{3,1},{4,6},{5,7},{6,4},{7,5},{8,10},{9,11},{10,... | collective-permute-start | bytes 32408 | tf_op jit(solution)/shard_map/ppermute | solution.py:438
  10.6 3.9 %collective-permute-start.2 = (f32[3,900]{1,0:T(4,128)S(1)}, f32[3,900]{1,0:T(4,128)S(1)}, u32[]{:S(2)}, u32[]{:S(2)}) collective-permute-start(f32[3,900]{1,0:T(4,128)S(1)} %reshape.9.op0_ref), channel_id=1, source_target_pairs={{0,1},{1,0},{2,3},{3,2},{4,5},{5,4},{6,7},{7,6},{8,9},{9,8},{10,11... | collective-permute-start | bytes 32408 | tf_op jit(solution)/shard_map/ppermute | solution.py:438
  11.4 3.1 %copy-start.4 = (f32[3,900]{1,0:T(4,128)}, f32[3,900]{1,0:T(4,128)S(1)}, u32[]{:S(2)}) copy-start(f32[3,900]{1,0:T(4,128)S(1)} %collective-permute-done.4.op3_ref) | copy-start | bytes 32404
  14.5 0.6 %copy-start.5 = (f32[3,900]{1,0:T(4,128)}, f32[3,900]{1,0:T(4,128)S(1)}, u32[]{:S(2)}) copy-start(f32[3,900]{1,0:T(4,128)S(1)} %collective-permute-done.3.op2_ref) | copy-start | bytes 32404
  14.5 0.6 %copy-start.6 = (f32[3,900]{1,0:T(4,128)}, f32[3,900]{1,0:T(4,128)S(1)}, u32[]{:S(2)}) copy-start(f32[3,900]{1,0:T(4,128)S(1)} %collective-permute-done.2.op1_ref) | copy-start | bytes 32404
  14.5 0.7 %copy-start = (f32[504,128]{1,0:T(8,128)}, f32[504,128]{1,0:T(8,128)S(1)}, u32[]{:S(2)}) copy-start(f32[504,128]{1,0:T(8,128)S(1)} %collective-permute-done.chip_ref) | copy-start | bytes 774148
  14.5 0.8 %copy-start.1 = (f32[504,128]{1,0:T(8,128)}, f32[504,128]{1,0:T(8,128)S(1)}, u32[]{:S(2)}) copy-start(f32[504,128]{1,0:T(8,128)S(1)} %collective-permute-done.1.next_ref) | copy-start | bytes 774148
  42.9 8.7 %collective-permute-start.5 = (f32[2,1000]{1,0:T(2,128)}, f32[2,1000]{1,0:T(2,128)S(1)}, u32[]{:S(2)}, u32[]{:S(2)}) collective-permute-start(f32[2,1000]{1,0:T(2,128)} %get-tuple-element.16), channel_id=1, source_target_pairs={{4,0},{8,4},{12,8},{16,12},{20,16},{24,20},{28,24},{32,28},{36,32}... | collective-permute-start | bytes 24008 | tf_op jit(solution)/shard_map/ppermute | solution.py:450
  51.6 0.6 %copy-start.7 = (f32[2,1000]{1,0:T(2,128)}, f32[2,1000]{1,0:T(2,128)S(1)}, u32[]{:S(2)}) copy-start(f32[2,1000]{1,0:T(2,128)S(1)} %collective-permute-done.5.in_ref) | copy-start | bytes 24004
